TPU v7x, 1024 devices: a whole 4x4x32 slice. The times are simulated.
1024 devices in a mesh: seq: 128 (over z, x), head: 8 (over y, core).
Axes of the slice: x: 4, y: 4, z: 32, core: 2. Of those that a mesh axis runs over, the one named last changes fastest.
Arguments:
- queries: bfloat16 [16384, 4096], P('seq', 'head'), may hold values from -150 to 150
- neighbours: bfloat16 [128, 128, 8, 448], P(None, 'seq', None, 'head'), may hold values from -6 to 6
- key_weight: bfloat16 [448, 4096], P(None, 'head'), may hold values from -0.25 to 0.25
- value_weight: bfloat16 [448, 4096], P(None, 'head'), may hold values from -0.25 to 0.25
- counts: int32 [256], P('seq'), may hold values from 1 to 4, as said below
- slot_map: int32 [128, 8], P('seq'), may hold values from 0 to 7, each once within a row
- d_attended: bfloat16 [16384, 4096], P('seq', 'head'), may hold values from -6 to 6
Outputs:
- attended: bfloat16 [16384, 4096], P('seq', 'head')
- d_queries: bfloat16 [16384, 4096], P('seq', 'head')
- d_neighbours: bfloat16 [128, 128, 8, 448], P(None, 'seq', None, 'head')
Inputs may be any that keep to these rules, and one draw needn't show every extreme that they name: `counts`: every span has at least one neighbour; some span has 4. `slot_map`: each row is a permutation; entry c * 4 + j names the slot that holds neighbour j of local span c, and only entries with j below the span's count are used.
All inputs are finite; a program needn't handle non-finite values.
Results may differ from a plain program's by a relative error of at most 0.03.
Values may be sent and summed in bfloat16 or wider, within the bound.
No kernel may reach another device: no remote copies, remote signals or barrier semaphores. Data moves between devices by JAX's collectives and lax.ppermute only.
A program may use at most 32 MiB of HBM per device.

v0:
```python
import jax
import jax.numpy as jnp
from jax import lax
from jax.sharding import PartitionSpec as P

HDIM = 128
SPAN = 64
NB_LEN = 128
MAX_NB = 4
CH_DEV = 2
SLOTS = 8


def present_table(count_row, slot_row):
    chosen = slot_row.reshape(CH_DEV, MAX_NB)
    ranks = jnp.arange(MAX_NB, dtype=jnp.int32)
    valid = ranks[None, :] < count_row[:, None]
    slot_ids = jnp.arange(SLOTS, dtype=jnp.int32)
    hits = valid[:, :, None] & (chosen[:, :, None] == slot_ids[None, None, :])
    return jnp.any(hits, axis=1)


def per_device(queries, neighbours, key_weight, value_weight, counts, slot_map, d_attended):
    total_rows = NB_LEN * SLOTS
    enc_local = neighbours.shape[3]
    width_local = key_weight.shape[1]
    heads_local = width_local // HDIM
    token_count = queries.shape[0]
    highest = lax.Precision.HIGHEST
    arrived = lax.all_to_all(neighbours, "seq", split_axis=0, concat_axis=1, tiled=True)
    flat_rows = arrived.reshape(total_rows, enc_local)
    portion = lax.all_gather(flat_rows, "head", axis=1, tiled=True)
    key_sum = jnp.dot(portion, key_weight, preferred_element_type=jnp.float32)
    value_sum = jnp.dot(portion, value_weight, preferred_element_type=jnp.float32)
    keys = key_sum.reshape(total_rows, heads_local, HDIM)
    values = value_sum.astype(jnp.bfloat16).reshape(total_rows, heads_local, HDIM)
    present = present_table(counts, slot_map[0])
    allowed = jnp.tile(jnp.repeat(present, SPAN, axis=0), (1, NB_LEN))
    factor = 1.0 / HDIM**0.5
    query_heads = queries.reshape(token_count, heads_local, HDIM)
    grad_heads = d_attended.reshape(token_count, heads_local, HDIM)
    scores = (
        jnp.einsum(
            "thd,rhd->htr",
            query_heads.astype(jnp.float32),
            keys,
            precision=highest,
            preferred_element_type=jnp.float32,
        )
        * factor
    )
    scores = jnp.where(allowed[None, :, :], scores, -jnp.inf)
    top = jnp.max(scores, axis=-1, keepdims=True)
    expo = jnp.exp(scores - top)
    probs = expo / jnp.sum(expo, axis=-1, keepdims=True)
    probs_b = probs.astype(jnp.bfloat16)
    attended = jnp.einsum("htr,rhd->thd", probs_b, values, preferred_element_type=jnp.float32)
    attended = attended.astype(jnp.bfloat16).reshape(token_count, width_local)
    dprobs = jnp.einsum("thd,rhd->htr", grad_heads, values, preferred_element_type=jnp.float32)
    inner = jnp.sum(probs * dprobs, axis=-1, keepdims=True)
    dscores = (probs * (dprobs - inner)).astype(jnp.bfloat16)
    d_queries = (
        jnp.einsum(
            "htr,rhd->thd",
            dscores.astype(jnp.float32),
            keys,
            precision=highest,
            preferred_element_type=jnp.float32,
        )
        * factor
    )
    d_queries = d_queries.astype(jnp.bfloat16).reshape(token_count, width_local)
    d_keys = (
        jnp.einsum("htr,thd->rhd", dscores, query_heads, preferred_element_type=jnp.float32)
        * factor
    )
    d_keys = d_keys.astype(jnp.bfloat16).reshape(total_rows, width_local)
    d_values = jnp.einsum("htr,thd->rhd", probs_b, grad_heads, preferred_element_type=jnp.float32)
    d_values = d_values.astype(jnp.bfloat16).reshape(total_rows, width_local)
    contract = (((1,), (1,)), ((), ()))
    partial_value = lax.dot_general(
        d_keys, key_weight, contract, preferred_element_type=jnp.float32
    )
    partial_value = partial_value + lax.dot_general(
        d_values, value_weight, contract, preferred_element_type=jnp.float32
    )
    summed = lax.psum(partial_value.astype(jnp.bfloat16), "head").astype(jnp.float32)
    own_part = lax.dynamic_slice_in_dim(summed, lax.axis_index("head") * enc_local, enc_local, 1)
    grad_rows = own_part.astype(jnp.bfloat16).reshape(1, NB_LEN, SLOTS, enc_local)
    d_neighbours = lax.all_to_all(grad_rows, "seq", split_axis=1, concat_axis=0, tiled=True)
    return (attended, d_queries, d_neighbours)


def solution(mesh):
    in_specs = (
        P("seq", "head"),
        P(None, "seq", None, "head"),
        P(None, "head"),
        P(None, "head"),
        P("seq"),
        P("seq", None),
        P("seq", "head"),
    )
    out_specs = (P("seq", "head"), P("seq", "head"), P(None, "seq", None, "head"))
    return jax.shard_map(
        per_device, mesh=mesh, in_specs=in_specs, out_specs=out_specs, check_vma=False
    )
```

profile of v0, /device:TPU:56, one launch (start us, length us, event | category | flops | bytes accessed | tf_op | source)
XLA Modules:
  0.0 253.7 jit_solution(9381826218336141485)
XLA Ops:
  7.2 1.2 copy.60
  8.4 0.9 reshape.93
  9.3 32.2 %all-to-all-start = ((bf16[128,2,224]{2,1,0:T(2,128)(2,1)}), bf16[128,2,224]{2,1,0:T(2,128)(2,1)S(1)}, u32[]{:S(2)}, u32[]{:S(2)}) async-start(bf16[128,2,224]{2,1,0:T(2,128)(2,1)} %reshape.93), calls=%async_computation | async-start | bytes 262144 | tf_op jit(solution)/shard_map/all_to_all | solution.py:30
  42.1 1.3 reduce.3
  44.6 1.0 copy.87
  45.6 1.0 copy.88
  46.7 26.3 %all-to-all-done = bf16[128,2,224]{2,1,0:T(2,128)(2,1)S(1)} async-done(((bf16[128,2,224]{2,1,0:T(2,128)(2,1)}), bf16[128,2,224]{2,1,0:T(2,128)(2,1)S(1)}, u32[]{:S(2)}, u32[]{:S(2)}) %all-to-all-start) | async-done | bytes 114720 | tf_op jit(solution)/shard_map/all_to_all | solution.py:30
  73.4 13.6 %all_gather.3 = bf16[1024,448]{0,1:T(8,128)(2,1)S(1)} all-gather(bf16[1024,56]{0,1:T(8,128)(2,1)S(1)} %copy.61), channel_id=1, replica_groups=mesh['seq'=128,'head'=8] {'head'}, dimensions={1}, use_global_device_ids=true | all-gather | bytes 1032192 | tf_op jit(solution)/shard_map/all_gather | solution.py:32
  87.0 1.7 convolution_convert_fusion.1
  89.5 1.8 fusion.18
  91.3 2.0 fusion.16
  93.3 3.6 %convolution_convert_fusion = bf16[4,1024,128]{1,2,0:T(8,128)(2,1)} fusion(bf16[128,4,128]{0,2,1:T(8,128)(2,1)S(1)} %bitcast.81, f32[4,128]{1,0:T(4,128)S(1)} %get-tuple-element.15, f32[4,1024,128]{2,1,0:T(8,128)} %copy-done.2, pred[128,1024]{0,1:T(8,128)(4,1)S(1)} %broadcast_bitcast_fusion), kind=kOutput, calls=%fused_computation.11 | convolution fusion | flops 137364992 | bytes 3409920 | tf_op jit(solution)/shard_map/htr,thd->rhd/dot_general | solution.py:78
  96.9 2.6 %fusion.1 = (f32[4,128]{1,0:T(4,128)S(1)}, f32[4,1024,128]{2,1,0:T(8,128)S(1)}) fusion(f32[4,128,1024]{1,2,0:T(8,128)} %get-tuple-element.16, f32[4,128]{1,0:T(4,128)S(1)} %get-tuple-element.15, bf16[1024,4,128]{0,2,1:T(8,128)(2,1)} %bitcast.84, bf16[128,4,128]{0,2,1:T(8,128)(2,1)S(1)} %bitcast.82), kind=kOutput, calls=%fused_computation.3 | convolution fusion | flops 135790080 | bytes 5378048 | tf_op jit(solution)/shard_map/thd,rhd->htr/dot_general | solution.py:59
  99.8 1.0 copy-done.1
  100.8 1.4 fusion.5
  102.2 2.3 copy.72
  104.5 2.0 fusion.19
  106.5 1.6 add_convert_fusion
  108.1 76.4 %all-reduce.2.cloned.1.call-done = bf16[1024,448]{0,1:T(8,128)(2,1)} async-done(((bf16[1024,448]{0,1:T(8,128)(2,1)}), bf16[1024,448]{0,1:T(8,128)(2,1)}) %all-reduce.2.cloned.1.call-update) | async-done | bytes 917520 | tf_op jit(solution)/shard_map/psum | solution.py:87
  184.5 0.9 convert_convert_fusion
  186.5 26.8 %all-to-all-start.1 = ((bf16[128,2,224]{2,1,0:T(2,128)(2,1)}), bf16[128,2,224]{2,1,0:T(2,128)(2,1)S(1)}, u32[]{:S(2)}, u32[]{:S(2)}) async-start(bf16[128,2,224]{2,1,0:T(2,128)(2,1)} %reshape.95), calls=%async_computation.1 | async-start | bytes 262144 | tf_op jit(solution)/shard_map/all_to_all | solution.py:90
  213.3 2.9 %convolution_convert_fusion.2 = bf16[4,128,128]{2,1,0:T(8,128)(2,1)S(1)} fusion(bf16[1024,4,128]{0,2,1:T(8,128)(2,1)} %bitcast.85, f32[4,128]{1,0:T(4,128)S(1)} %get-tuple-element.15, f32[4,1024,128]{2,1,0:T(8,128)} %copy-done.2, pred[128,1024]{0,1:T(8,128)(4,1)S(1)} %broadcast_bitcast_fusion), kind=kOutput, calls=%fused_computation.16 | convolution fusion | flops 136906240 | bytes 3409920 | tf_op jit(solution)/shard_map/htr,rhd->thd/dot_general | solution.py:57
  217.0 2.3 fusion.6
  220.1 25.7 %all-to-all-done.1 = bf16[128,2,224]{2,1,0:T(2,128)(2,1)S(1)} async-done(((bf16[128,2,224]{2,1,0:T(2,128)(2,1)}), bf16[128,2,224]{2,1,0:T(2,128)(2,1)S(1)}, u32[]{:S(2)}, u32[]{:S(2)}) %all-to-all-start.1) | async-done | bytes 114720 | tf_op jit(solution)/shard_map/all_to_all | solution.py:90
  (35 shorter events, 6.8 us)
Async XLA Ops:
  7.2 81.6 %copy-start = (bf16[448,512]{1,0:T(8,128)(2,1)S(1)}, bf16[448,512]{1,0:T(8,128)(2,1)}, u32[]{:S(2)}) copy-start(bf16[448,512]{1,0:T(8,128)(2,1)} %param.9) | copy-start | bytes 1376260
  7.2 79.8 %copy-start.5 = (bf16[448,512]{1,0:T(8,128)(2,1)S(1)}, bf16[448,512]{1,0:T(8,128)(2,1)}, u32[]{:S(2)}) copy-start(bf16[448,512]{1,0:T(8,128)(2,1)} %param.10) | copy-start | bytes 1376260
  9.3 63.8 %all-to-all-start = ((bf16[128,2,224]{2,1,0:T(2,128)(2,1)}), bf16[128,2,224]{2,1,0:T(2,128)(2,1)S(1)}, u32[]{:S(2)}, u32[]{:S(2)}) async-start(bf16[128,2,224]{2,1,0:T(2,128)(2,1)} %reshape.93), calls=%async_computation | async-start | bytes 262144 | tf_op jit(solution)/shard_map/all_to_all | solution.py:30
  41.5 143.0 %all-reduce.2.cloned.1.call-start = ((), (), s32[]{:S(2)}) async-start(), calls=%async_computation.2 | async-start | bytes 1835008 | tf_op jit(solution)/shard_map/psum | solution.py:87
  91.3 2.0 copy-start.2
  96.9 2.6 %copy-start.3 = (f32[4,128,1024]{1,2,0:T(8,128)S(1)}, f32[4,128,1024]{1,2,0:T(8,128)}, u32[]{:S(2)}) copy-start(f32[4,128,1024]{1,2,0:T(8,128)} %get-tuple-element.16) | copy-start | bytes 6291460
  99.8 1.0 copy-start.1
  104.5 2.0 copy-start.4
  104.5 2.0 copy-start.6
  186.5 59.3 %all-to-all-start.1 = ((bf16[128,2,224]{2,1,0:T(2,128)(2,1)}), bf16[128,2,224]{2,1,0:T(2,128)(2,1)S(1)}, u32[]{:S(2)}, u32[]{:S(2)}) async-start(bf16[128,2,224]{2,1,0:T(2,128)(2,1)} %reshape.95), calls=%async_computation.1 | async-start | bytes 262144 | tf_op jit(solution)/shard_map/all_to_all | solution.py:90
Sparse Core Ops, SparseCore 0:
  108.2 76.1 all-reduce.1
where the time goes:
time: 254 us
  waiting for transfers between devices  128 us (50%)
  starting transfers between devices  59 us (23%)
  matrix products  20.8 us (8%)
  between operations  14.2 us (6%)
  blocking collectives  13.6 us (5%)
  local copies, waits for them, and re-layouts  12.3 us (5%)
  other arithmetic  5.3 us (2%)
    psum x1, waiting for transfers between devices, per_device(): lax.psum(partial_value.astype(jnp.bfloat16), 'head').astype(jnp.float32)  76.4 us
    all_to_all x1, starting transfers between devices, per_device(): lax.all_to_all(neighbours, 'seq', split_axis=0, concat_axis=1, tiled=True)  32.2 us
    all_to_all x1, starting transfers between devices, per_device(): lax.all_to_all(grad_rows, 'seq', split_axis=1, concat_axis=0, tiled=True)  26.8 us
    all_to_all x1, waiting for transfers between devices, per_device(): lax.all_to_all(neighbours, 'seq', split_axis=0, concat_axis=1, tiled=True)  26.3 us
    all_to_all x1, waiting for transfers between devices, per_device(): lax.all_to_all(grad_rows, 'seq', split_axis=1, concat_axis=0, tiled=True)  25.7 us
    all_gather x1, blocking collectives, per_device(): portion = lax.all_gather(flat_rows, 'head', axis=1, tiled=True)  13.6 us
    unnamed x24, local copies, waits for them, and re-layouts  7.27 us
  transfers between devices with their start and end apart: 3, of which 3 were waited for; matrix products, arithmetic and copies ran while one was open for 5% of the time, Pallas kernels for 0%

commit v1 on v0

v1 whole, which is shorter than its diff:
```python
import jax
import jax.numpy as jnp
from jax import lax
from jax.experimental import pallas as pl
from jax.experimental.pallas import tpu as pltpu
from jax.sharding import PartitionSpec as P

HDIM = 128
SPAN = 64
NB_LEN = 128
MAX_NB = 4
CH_DEV = 2
SLOTS = 8
LANES = 128
BF = jnp.bfloat16
F32 = jnp.float32
VMEM_LIMIT = 48 * 1024 * 1024


def vmem():
    return pl.BlockSpec(memory_space=pltpu.VMEM)


def smem():
    return pl.BlockSpec(memory_space=pltpu.SMEM)


def to_messages(flat, out_ref):
    blocks = out_ref.shape[1]
    extra = blocks * LANES - flat.shape[0]
    turned = jnp.concatenate([flat, jnp.zeros((extra, flat.shape[1]), flat.dtype)], axis=0).T
    turned = turned.astype(BF)
    for i in range(blocks):
        out_ref[:, i, :] = turned[:, i * LANES : (i + 1) * LANES]


def pack_kernel(flat_ref, out_ref):
    to_messages(flat_ref[...], out_ref)


def unpack_kernel(in_ref, out_ref):
    parts = [in_ref[:, i, :] for i in range(in_ref.shape[1])]
    out_ref[...] = jnp.concatenate(parts, axis=1).T[: out_ref.shape[0]]


def sum_pack_kernel(parts_ref, out_ref):
    total = parts_ref[0].astype(F32)
    for i in range(1, parts_ref.shape[0]):
        total = total + parts_ref[i].astype(F32)
    to_messages(total.astype(BF), out_ref)


def attend_kernel(counts_ref, slots_ref, rows_ref, up_ref, down_ref, q_ref, g_ref, att_ref, dq_ref, part_ref, x_ref, dkv_ref):
    n_head = rows_ref.shape[0]
    chunk = rows_ref.shape[2]
    heads = q_ref.shape[1] // HDIM
    span_rows = MAX_NB * NB_LEN
    factor = 1.0 / HDIM**0.5
    for j in range(SLOTS):
        slot = slots_ref[0, j]
        for b in range(n_head):
            x_ref[b * chunk : (b + 1) * chunk, j * NB_LEN : (j + 1) * NB_LEN] = rows_ref[b, slot]
    lane = lax.broadcasted_iota(jnp.int32, (SPAN, span_rows), 1)
    nt = (((1,), (1,)), ((), ()))
    tn = (((0,), (0,)), ((), ()))
    for h in range(heads):
        lo, hi = h * HDIM, (h + 1) * HDIM
        kv = jnp.dot(up_ref[2 * lo : 2 * hi, :], x_ref[...], preferred_element_type=F32)
        key = kv[:HDIM]
        value = kv[HDIM:].astype(BF)
        key_hi = key.astype(BF)
        key_lo = (key - key_hi.astype(F32)).astype(BF)
        key_two = jnp.concatenate([key_hi, key_lo], axis=0)
        for c in range(CH_DEV):
            tok = slice(c * SPAN, (c + 1) * SPAN)
            own = slice(c * span_rows, (c + 1) * span_rows)
            query = q_ref[tok, lo:hi]
            grad = g_ref[tok, lo:hi]
            k_c = key_two[:, own]
            v_c = value[:, own]
            scores = jnp.dot(jnp.concatenate([query, query], axis=1), k_c, preferred_element_type=F32) * factor
            scores = jnp.where(lane < counts_ref[c] * NB_LEN, scores, -jnp.inf)
            top = jnp.max(scores, axis=1, keepdims=True)
            expo = jnp.exp(scores - top)
            probs = expo * (1.0 / jnp.sum(expo, axis=1, keepdims=True))
            probs_b = probs.astype(BF)
            dprobs = jnp.dot(grad, v_c, preferred_element_type=F32)
            inner = jnp.sum(probs * dprobs, axis=1, keepdims=True)
            dscores = (probs * (dprobs - inner)).astype(BF)
            att = lax.dot_general(probs_b, v_c, nt, preferred_element_type=F32)
            att_ref[tok, lo:hi] = att.astype(BF)
            dq = lax.dot_general(dscores, k_c, nt, preferred_element_type=F32)
            dq_ref[tok, lo:hi] = ((dq[:, :HDIM] + dq[:, HDIM:]) * factor).astype(BF)
            dk = lax.dot_general(query, dscores, tn, preferred_element_type=F32) * factor
            dv = lax.dot_general(grad, probs_b, tn, preferred_element_type=F32)
            dkv_ref[2 * lo : 2 * lo + HDIM, own] = dk.astype(BF)
            dkv_ref[2 * lo + HDIM : 2 * hi, own] = dv.astype(BF)
    part = jnp.dot(down_ref[...], dkv_ref[...], preferred_element_type=F32).astype(BF)
    for j in range(SLOTS):
        slot = slots_ref[0, j]
        for b in range(n_head):
            part_ref[b, slot] = part[b * chunk : (b + 1) * chunk, j * NB_LEN : (j + 1) * NB_LEN]


def params():
    return pltpu.CompilerParams(vmem_limit_bytes=VMEM_LIMIT)


def per_device(queries, neighbours, key_weight, value_weight, counts, slot_map, d_attended):
    n_seq = neighbours.shape[0]
    chunk = neighbours.shape[3]
    enc, width = key_weight.shape
    n_head = enc // chunk
    heads = width // HDIM
    flat = SLOTS * chunk
    blocks = -(-flat // LANES)
    messages = jax.ShapeDtypeStruct((n_seq, blocks, LANES), BF)

    turned = neighbours.transpose(1, 2, 3, 0).reshape(flat, n_seq)
    out = pl.pallas_call(pack_kernel, out_shape=messages, in_specs=[vmem()], out_specs=vmem(), compiler_params=params(), name="pack")(turned)
    arrived = lax.all_to_all(out, "seq", split_axis=0, concat_axis=0, tiled=True)
    both = jnp.stack([key_weight.reshape(enc, heads, HDIM), value_weight.reshape(enc, heads, HDIM)], axis=2)
    down = both.reshape(enc, 2 * width)
    up = down.T
    rows = pl.pallas_call(
        unpack_kernel, out_shape=jax.ShapeDtypeStruct((flat, NB_LEN), BF), in_specs=[vmem()], out_specs=vmem(), compiler_params=params(), name="unpack"
    )(arrived)
    rows = lax.all_gather(rows, "head", axis=0, tiled=True).reshape(n_head, SLOTS, chunk, NB_LEN)
    attended, d_queries, partial_value = pl.pallas_call(
        attend_kernel,
        out_shape=(
            jax.ShapeDtypeStruct(queries.shape, BF),
            jax.ShapeDtypeStruct(queries.shape, BF),
            jax.ShapeDtypeStruct((n_head, SLOTS, chunk, NB_LEN), BF),
        ),
        in_specs=[smem(), smem()] + [vmem()] * 5,
        out_specs=(vmem(), vmem(), vmem()),
        scratch_shapes=[pltpu.VMEM((enc, SLOTS * NB_LEN), BF), pltpu.VMEM((2 * width, SLOTS * NB_LEN), BF)],
        compiler_params=params(),
        name="attend",
    )(counts, slot_map, rows, up, down, queries, d_attended)
    pieces = lax.all_to_all(partial_value.reshape(n_head, flat, NB_LEN), "head", split_axis=0, concat_axis=0, tiled=True)
    back = pl.pallas_call(
        sum_pack_kernel, out_shape=jax.ShapeDtypeStruct((NB_LEN, blocks, LANES), BF), in_specs=[vmem()], out_specs=vmem(), compiler_params=params(), name="sum_pack"
    )(pieces)
    home = lax.all_to_all(back, "seq", split_axis=0, concat_axis=0, tiled=True)
    grad = pl.pallas_call(
        unpack_kernel, out_shape=jax.ShapeDtypeStruct((flat, n_seq), BF), in_specs=[vmem()], out_specs=vmem(), compiler_params=params(), name="unpack_back"
    )(home)
    d_neighbours = grad.reshape(1, SLOTS, chunk, n_seq).transpose(3, 0, 1, 2)
    return (attended, d_queries, d_neighbours)


def solution(mesh):
    in_specs = (
        P("seq", "head"),
        P(None, "seq", None, "head"),
        P(None, "head"),
        P(None, "head"),
        P("seq"),
        P("seq", None),
        P("seq", "head"),
    )
    out_specs = (P("seq", "head"), P("seq", "head"), P(None, "seq", None, "head"))
    return jax.shard_map(
        per_device, mesh=mesh, in_specs=in_specs, out_specs=out_specs, check_vma=False
    )
```

time: 254 us -> 145 us (0.57)
  the two profiles are of different devices: /device:TPU:56 before, /device:TPU:32 now
where the time goes in v1:
time: 145 us
  blocking collectives  69.6 us (48%)
  starting transfers between devices  32.2 us (22%)
  waiting for transfers between devices  25.1 us (17%)
  Pallas kernels  10 us (7%)
  local copies, waits for them, and re-layouts  5.12 us (4%)
  other arithmetic  2.08 us (1%)
    all_to_all x1, blocking collectives, per_device(): home = lax.all_to_all(back, 'seq', split_axis=0, concat_axis=0, tiled=True)  37.2 us
    all_to_all x1, starting transfers between devices, per_device(): lax.all_to_all(out, 'seq', split_axis=0, concat_axis=0, tiled=True)  32.2 us
    all_to_all x1, waiting for transfers between devices, per_device(): lax.all_to_all(out, 'seq', split_axis=0, concat_axis=0, tiled=True)  25.1 us
    all_to_all x1, blocking collectives, per_device(): lax.all_to_all(partial_value.reshape(n_head, flat, NB_LEN), 'head', split...  18.2 us
    all_gather x1, blocking collectives, per_device(): lax.all_gather(rows, 'head', axis=0, tiled=True)  14.1 us
    pallas_call x1, Pallas kernels, per_device(): pl.pallas_call(attend_kernel, out_shape=(jax.ShapeDtypeStruct(queries.sha...  7.1 us
    another operation x2, local copies, waits for them, and re-layouts, per_device(): jnp.stack([key_weight.reshape(enc, heads, HDIM), value_weight.reshape(enc...  3.01 us
  transfers between devices with their start and end apart: 1, of which 1 were waited for; matrix products, arithmetic and copies ran while one was open for 4% of the time, Pallas kernels for 0%

profile of v1, /device:TPU:32, one launch (start us, length us, event | category | flops | bytes accessed | tf_op | source)
XLA Modules:
  0.0 144.9 jit_solution(119039576219761219)
XLA Ops:
  0.6 0.0 copy-start.2
  0.6 0.9 copy-done.2
  1.5 1.0 pack.1
  2.6 32.2 %all-to-all-start = ((bf16[128,4,128]{2,1,0:T(4,128)(2,1)}), bf16[128,4,128]{2,1,0:T(4,128)(2,1)S(1)}, u32[]{:S(2)}, u32[]{:S(2)}) async-start(bf16[128,4,128]{2,1,0:T(4,128)(2,1)} %pack.1), calls=%async_computation | async-start | bytes 262144 | tf_op jit(solution)/shard_map/all_to_all | solution.py:121
  34.8 2.7 %stack_reshape.8 = bf16[448,4,1,128]{3,2,1,0:T(2,128)(2,1)S(1)} reshape(bf16[448,512]{1,0:T(8,128)(2,1)} %param.9) | data formatting | bytes 917504 | tf_op jit(solution)/shard_map/stack;reshape | solution.py:122
  37.6 0.0 copy-done.5
  37.6 0.3 stack_reshape.9
  37.9 2.1 %pad_maximum_fusion = bf16[448,4,2,128]{3,2,1,0:T(2,128)(2,1)S(1)} fusion(bf16[448,4,1,128]{3,2,1,0:T(2,128)(2,1)S(1)} %stack_reshape.9, bf16[448,4,1,128]{3,2,1,0:T(2,128)(2,1)S(1)} %stack_reshape.8), kind=kLoop, calls=%fused_computation | loop fusion | flops 1835008 | bytes 1835008 | tf_op jit(solution)/shard_map/stack | solution.py:122
  39.9 0.7 reshape.23.down_ref
  40.6 0.5 copy.12.up_ref
  41.1 0.0 copy-start
  41.2 0.0 copy-start.1
  41.2 0.0 copy-start.3
  41.2 0.0 copy-start.4
  41.2 25.1 %all-to-all-done.in_ref = bf16[128,4,128]{2,1,0:T(4,128)(2,1)S(1)} async-done(((bf16[128,4,128]{2,1,0:T(4,128)(2,1)}), bf16[128,4,128]{2,1,0:T(4,128)(2,1)S(1)}, u32[]{:S(2)}, u32[]{:S(2)}) %all-to-all-start) | async-done | bytes 131104 | tf_op jit(solution)/shard_map/all_to_all | solution.py:121
  66.3 0.3 unpack.1
  66.6 14.1 %all_gather.3 = bf16[3584,128]{1,0:T(8,128)(2,1)S(1)} all-gather(bf16[448,128]{1,0:T(8,128)(2,1)S(1)} %unpack.1), channel_id=1, replica_groups=mesh['seq'=128,'head'=8] {'head'}, dimensions={0}, use_global_device_ids=true | all-gather | bytes 1032192 | tf_op jit(solution)/shard_map/all_gather | solution.py:128
  80.7 0.0 copy-done
  80.7 0.0 copy-done.1
  80.8 7.1 %attend.1 = (bf16[128,512]{1,0:T(8,128)(2,1)}, bf16[128,512]{1,0:T(8,128)(2,1)}, bf16[8,8,56,128]{3,2,1,0:T(8,128)(2,1)S(1)}) custom-call(s32[2]{0:T(128)S(1)} %copy-done.3, s32[1,8]{1,0:T(1,128)S(1)} %copy-done.4, bf16[8,8,56,128]{3,2,1,0:T(8,128)(2,1)S(1)} %bitcast.10, bf16[1024,448]{1,0:T(8,128)(2,1)S(1)} %copy.12.up_ref, ...), custom_call_target="tpu_custom_call" | custom-call | tf_op jit(solution)/shard_map/attend/pallas_call | solution.py:129
  87.9 18.2 %all_to_all.15.parts_ref = bf16[8,448,128]{2,1,0:T(8,128)(2,1)S(1)} all-to-all(bf16[8,448,128]{2,1,0:T(8,128)(2,1)S(1)} %bitcast.11), channel_id=1, replica_groups=mesh['seq'=128,'head'=8] {'head'}, dimensions={0} | all-to-all | bytes 1835008 | tf_op jit(solution)/shard_map/all_to_all | solution.py:142
  106.1 0.6 sum_pack.1
  106.7 37.2 %all_to_all.16.in_ref = bf16[128,4,128]{2,1,0:T(4,128)(2,1)S(1)} all-to-all(bf16[128,4,128]{2,1,0:T(4,128)(2,1)S(1)} %sum_pack.1), channel_id=1, replica_groups=mesh['seq'=128,'head'=8] {'seq'}, dimensions={0} | all-to-all | bytes 262144 | tf_op jit(solution)/shard_map/all_to_all | solution.py:146
  143.9 0.9 unpack_back.1
  (3 shorter events, 0.0 us)
Async XLA Ops:
  0.6 0.9 copy-start.2
  1.5 36.0 %copy-start.5 = (bf16[448,512]{1,0:T(8,128)(2,1)S(1)}, bf16[448,512]{1,0:T(8,128)(2,1)}, u32[]{:S(2)}) copy-start(bf16[448,512]{1,0:T(8,128)(2,1)} %param.10) | copy-start | bytes 1376260
  2.6 63.8 %all-to-all-start = ((bf16[128,4,128]{2,1,0:T(4,128)(2,1)}), bf16[128,4,128]{2,1,0:T(4,128)(2,1)S(1)}, u32[]{:S(2)}, u32[]{:S(2)}) async-start(bf16[128,4,128]{2,1,0:T(4,128)(2,1)} %pack.1), calls=%async_computation | async-start | bytes 262144 | tf_op jit(solution)/shard_map/all_to_all | solution.py:121
  41.1 39.6 %copy-start = (bf16[128,512]{1,0:T(8,128)(2,1)S(1)}, bf16[128,512]{1,0:T(8,128)(2,1)}, u32[]{:S(2)}) copy-start(bf16[128,512]{1,0:T(8,128)(2,1)} %q_ref.1) | copy-start | bytes 393220
  41.2 39.6 %copy-start.1 = (bf16[128,512]{1,0:T(8,128)(2,1)S(1)}, bf16[128,512]{1,0:T(8,128)(2,1)}, u32[]{:S(2)}) copy-start(bf16[128,512]{1,0:T(8,128)(2,1)} %g_ref.1) | copy-start | bytes 393220
  41.2 39.6 %copy-start.3 = (s32[2]{0:T(128)S(1)}, s32[2]{0:T(128)}, u32[]{:S(2)}) copy-start(s32[2]{0:T(128)} %counts_ref.1) | copy-start | bytes 28
  41.2 39.6 %copy-start.4 = (s32[1,8]{1,0:T(1,128)S(1)}, s32[1,8]{1,0:T(1,128)}, u32[]{:S(2)}) copy-start(s32[1,8]{1,0:T(1,128)} %slots_ref.1) | copy-start | bytes 100

commit v2 on v1

v2 whole, which is shorter than its diff:
```python
import jax
import jax.numpy as jnp
from jax import lax
from jax.experimental import pallas as pl
from jax.experimental.pallas import tpu as pltpu
from jax.sharding import Mesh, PartitionSpec as P

HDIM = 128
SPAN = 64
NB_LEN = 128
MAX_NB = 4
CH_DEV = 2
SLOTS = 8
LANES = 128
X_CHIPS = 4
CORES = 2
FIRST_IN = 24
FIRST_OUT = 16
BF = jnp.bfloat16
F32 = jnp.float32
VMEM_LIMIT = 48 * 1024 * 1024


def vmem():
    return pl.BlockSpec(memory_space=pltpu.VMEM)


def smem():
    return pl.BlockSpec(memory_space=pltpu.SMEM)


def to_rows(flat):
    extra = -flat.shape[0] % LANES
    return jnp.concatenate([flat, jnp.zeros((extra, flat.shape[1]), flat.dtype)], axis=0).T


def swapped(n, first):
    run = first & -first if first else n
    return [(slice(k ^ first, (k ^ first) + run), slice(k, k + run)) for k in range(0, n, run)]


def scaled(run, by):
    return slice(run.start * by, run.stop * by)


def pack_kernel(flat_ref, out_ref):
    turned = to_rows(flat_ref[...])
    n_x = X_CHIPS
    for src, dst in swapped(out_ref.shape[0] // n_x, FIRST_IN):
        for i in range(out_ref.shape[1]):
            out_ref[scaled(dst, n_x), i, :] = turned[scaled(src, n_x), i * LANES : (i + 1) * LANES]


def unpack_kernel(in_ref, out_ref):
    n_x = X_CHIPS
    runs = swapped(in_ref.shape[0] // n_x, FIRST_OUT)
    parts = [jnp.concatenate([in_ref[scaled(src, n_x), i, :] for src, _ in runs], axis=0) for i in range(in_ref.shape[1])]
    out_ref[...] = jnp.concatenate(parts, axis=1).T[: out_ref.shape[0]]


def spread_kernel(in_ref, out_ref):
    for x in range(out_ref.shape[0]):
        own = in_ref[:, x]
        for y in range(out_ref.shape[1]):
            out_ref[x, y] = own


def turn_kernel(in_ref, out_ref):
    n_x, n_y, _, blocks, _ = in_ref.shape
    for y in range(n_y):
        rows = [jnp.concatenate([in_ref[x, y, :, i, :] for x in range(n_x)], axis=0) for i in range(blocks)]
        out_ref[y] = jnp.concatenate(rows, axis=1).T[: out_ref.shape[1]]


def join_kernel(keep_ref, got_ref, out_ref):
    n_x, n_y, n_z, blocks, _ = out_ref.shape
    for y in range(n_y):
        turned = to_rows((keep_ref[y].astype(F32) + got_ref[y].astype(F32)).astype(BF))
        for x in range(n_x):
            for i in range(blocks):
                out_ref[x, y, :, i, :] = turned[x * n_z : (x + 1) * n_z, i * LANES : (i + 1) * LANES]


def sum_kernel(in_ref, out_ref):
    n_x, n_y = in_ref.shape[:2]
    for x in range(n_x):
        total = in_ref[x, 0].astype(F32)
        for y in range(1, n_y):
            total = total + in_ref[x, y].astype(F32)
        total = total.astype(BF)
        for src, dst in swapped(out_ref.shape[0], FIRST_IN ^ FIRST_OUT):
            out_ref[dst, x] = total[src]


def attend_kernel(
    counts_ref, slots_ref, core_ref, rows_ref, wk_ref, wv_ref, q_ref, g_ref, att_ref, dq_ref, keep_ref, send_ref, x_ref, dk_ref, dv_ref, part_ref
):
    n_core, n_y, _, chunk, _ = rows_ref.shape
    heads = q_ref.shape[1] // HDIM
    span_rows = MAX_NB * NB_LEN
    factor = 1.0 / HDIM**0.5
    for j in range(SLOTS):
        slot = slots_ref[0, j]
        for b in range(n_core * n_y):
            x_ref[b * chunk : (b + 1) * chunk, j * NB_LEN : (j + 1) * NB_LEN] = rows_ref[b % n_core, b // n_core, slot]
    lane = lax.broadcasted_iota(jnp.int32, (SPAN, span_rows), 1)
    nt = (((1,), (1,)), ((), ()))
    tn = (((0,), (0,)), ((), ()))
    for h in range(heads):
        lo, hi = h * HDIM, (h + 1) * HDIM
        key = lax.dot_general(wk_ref[:, lo:hi], x_ref[...], tn, preferred_element_type=F32)
        value = lax.dot_general(wv_ref[:, lo:hi], x_ref[...], tn, preferred_element_type=F32).astype(BF)
        key_hi = key.astype(BF)
        key_lo = (key - key_hi.astype(F32)).astype(BF)
        key_two = jnp.concatenate([key_hi, key_lo], axis=0)
        for c in range(CH_DEV):
            tok = slice(c * SPAN, (c + 1) * SPAN)
            own = slice(c * span_rows, (c + 1) * span_rows)
            query = q_ref[tok, lo:hi]
            grad = g_ref[tok, lo:hi]
            k_c = key_two[:, own]
            v_c = value[:, own]
            scores = jnp.dot(jnp.concatenate([query, query], axis=1), k_c, preferred_element_type=F32) * factor
            scores = jnp.where(lane < counts_ref[c] * NB_LEN, scores, -jnp.inf)
            top = jnp.max(scores, axis=1, keepdims=True)
            expo = jnp.exp(scores - top)
            probs = expo * (1.0 / jnp.sum(expo, axis=1, keepdims=True))
            probs_b = probs.astype(BF)
            dprobs = jnp.dot(grad, v_c, preferred_element_type=F32)
            inner = jnp.sum(probs * dprobs, axis=1, keepdims=True)
            dscores = (probs * (dprobs - inner)).astype(BF)
            att = lax.dot_general(probs_b, v_c, nt, preferred_element_type=F32)
            att_ref[tok, lo:hi] = att.astype(BF)
            dq = lax.dot_general(dscores, k_c, nt, preferred_element_type=F32)
            dq_ref[tok, lo:hi] = ((dq[:, :HDIM] + dq[:, HDIM:]) * factor).astype(BF)
            dk = lax.dot_general(query, dscores, tn, preferred_element_type=F32) * factor
            dv = lax.dot_general(grad, probs_b, tn, preferred_element_type=F32)
            dk_ref[lo:hi, own] = dk.astype(BF)
            dv_ref[lo:hi, own] = dv.astype(BF)
    part = jnp.dot(wk_ref[...], dk_ref[...], preferred_element_type=F32)
    part = (part + jnp.dot(wv_ref[...], dv_ref[...], preferred_element_type=F32)).astype(BF)
    for b in range(n_core * n_y):
        part_ref[b] = part[b * chunk : (b + 1) * chunk]
    core = core_ref[0]
    for j in range(SLOTS):
        slot = slots_ref[0, j]
        for y in range(n_y):
            keep_ref[y, slot] = part_ref[y * n_core + core, :, j * NB_LEN : (j + 1) * NB_LEN]
            send_ref[y, slot] = part_ref[y * n_core + 1 - core, :, j * NB_LEN : (j + 1) * NB_LEN]


def call(kernel, outs, n_in, name, small=0, scratch=()):
    one = isinstance(outs, jax.ShapeDtypeStruct)
    return pl.pallas_call(
        kernel,
        out_shape=outs,
        in_specs=[smem()] * small + [vmem()] * n_in,
        out_specs=vmem() if one else tuple(vmem() for _ in outs),
        scratch_shapes=scratch,
        compiler_params=pltpu.CompilerParams(vmem_limit_bytes=VMEM_LIMIT),
        name=name,
    )


def exchange(messages, first):
    n_z = messages.shape[0]
    return lax.all_to_all(
        messages, "z", split_axis=0, concat_axis=0, axis_index_groups=[[k ^ first for k in range(n_z)]], tiled=True
    )


def per_device(queries, neighbours, key_weight, value_weight, counts, slot_map, d_attended):
    n_z, n_x, n_y, n_core = (lax.axis_size(a) for a in ("z", "x", "y", "core"))
    n_seq = n_z * n_x
    chunk = neighbours.shape[3]
    enc, width = key_weight.shape
    flat = SLOTS * chunk
    blocks = -(-flat // LANES)
    rows = SLOTS * NB_LEN

    def shape(*dims):
        return jax.ShapeDtypeStruct(dims, BF)

    turned = neighbours.transpose(1, 2, 3, 0).reshape(flat, n_seq)
    core, turned = lax.optimization_barrier((lax.axis_index("core").reshape(1), turned))
    out = call(pack_kernel, shape(n_seq, blocks, LANES), 1, "pack")(turned)
    out = exchange(out.reshape(n_z, n_x * blocks, LANES), FIRST_IN)
    out = call(spread_kernel, shape(n_x, n_y, n_z, blocks, LANES), 1, "spread")(out.reshape(n_z, n_x, blocks, LANES))
    out = lax.all_to_all(out.reshape(n_x * n_y, n_z, blocks, LANES), ("x", "y"), split_axis=0, concat_axis=0, tiled=True)
    out = call(turn_kernel, shape(n_y, flat, NB_LEN), 1, "turn")(out.reshape(n_x, n_y, n_z, blocks, LANES))
    out = lax.all_gather(out, "core", axis=0).reshape(n_core, n_y, SLOTS, chunk, NB_LEN)
    half = shape(n_y, SLOTS, chunk, NB_LEN)
    attended, d_queries, keep, send = call(
        attend_kernel,
        (shape(*queries.shape), shape(*queries.shape), half, half),
        5,
        "attend",
        small=3,
        scratch=(
            pltpu.VMEM((enc, rows), BF),
            pltpu.VMEM((width, rows), BF),
            pltpu.VMEM((width, rows), BF),
            pltpu.VMEM((n_core * n_y, chunk, rows), BF),
        ),
    )(counts, slot_map, core, out, key_weight, value_weight, queries, d_attended)
    got = lax.ppermute(send, "core", [(0, 1), (1, 0)])
    back = call(join_kernel, shape(n_x, n_y, n_z, blocks, LANES), 2, "join")(keep.reshape(n_y, flat, NB_LEN), got.reshape(n_y, flat, NB_LEN))
    back = lax.all_to_all(back.reshape(n_x * n_y, n_z, blocks, LANES), ("x", "y"), split_axis=0, concat_axis=0, tiled=True)
    back = call(sum_kernel, shape(n_z, n_x, blocks, LANES), 1, "sum")(back.reshape(n_x, n_y, n_z, blocks, LANES))
    home = exchange(back.reshape(n_z, n_x * blocks, LANES), FIRST_OUT)
    grad = call(unpack_kernel, shape(flat, n_seq), 1, "unpack")(home.reshape(n_seq, blocks, LANES))
    d_neighbours = grad.reshape(1, SLOTS, chunk, n_seq).transpose(3, 0, 1, 2)
    return (attended, d_queries, d_neighbours)


def solution(mesh):
    n_seq, n_head = mesh.devices.shape
    fine = Mesh(mesh.devices.reshape(n_seq // X_CHIPS, X_CHIPS, n_head // CORES, CORES), ("z", "x", "y", "core"))
    seq, head = ("z", "x"), ("y", "core")
    in_specs = (
        P(seq, head),
        P(None, seq, None, head),
        P(None, head),
        P(None, head),
        P(seq),
        P(seq, None),
        P(seq, head),
    )
    out_specs = (P(seq, head), P(seq, head), P(None, seq, None, head))
    return jax.shard_map(
        per_device, mesh=fine, in_specs=in_specs, out_specs=out_specs, check_vma=False
    )
```

time: 145 us -> 136 us (0.938)
  the two profiles are of different devices: /device:TPU:32 before, /device:TPU:1 now
where the time goes in v2:
time: 136 us
  blocking collectives  118 us (87%)
  Pallas kernels  11.9 us (9%)
  starting transfers between devices  2.27 us (2%)
  local copies, waits for them, and re-layouts  1.55 us (1%)
  waiting for transfers between devices  1.42 us (1%)
    all_to_all x2, blocking collectives, exchange(): lax.all_to_all(messages, 'z', split_axis=0, concat_axis=0, axis_index_gro...  83.2 us
    all_to_all x1, blocking collectives, per_device(): lax.all_to_all(out.reshape(n_x * n_y, n_z, blocks, LANES), ('x', 'y'), sp...  15.8 us
    all_to_all x1, blocking collectives, per_device(): lax.all_to_all(back.reshape(n_x * n_y, n_z, blocks, LANES), ('x', 'y'), s...  13.3 us
    pallas_call x1, Pallas kernels, per_device(): call(attend_kernel, (shape(*queries.shape), shape(*queries.shape), half,...  7.83 us
    all_gather x1, blocking collectives, per_device(): lax.all_gather(out, 'core', axis=0)  5.44 us
  transfers between devices with their start and end apart: 1, of which 1 were waited for; matrix products, arithmetic and copies ran while one was open for 0% of the time, Pallas kernels for 0%

profile of v2, /device:TPU:1, one launch (start us, length us, event | category | flops | bytes accessed | tf_op | source)
XLA Modules:
  0.0 135.7 jit_solution(9451335813060843633)
XLA Ops:
  0.6 0.0 copy-start.4
  0.6 0.9 copy-done.4
  1.5 0.4 pack.1
  1.9 49.5 %all_to_all.20 = bf16[32,16,128]{2,1,0:T(8,128)(2,1)S(1)} all-to-all(bf16[32,16,128]{2,1,0:T(8,128)(2,1)S(1)} %bitcast.26), channel_id=1, replica_groups={{768,800,832,864,896,928,960,992,512,544,576,608,640,672,704,736,256,28..., dimensions={0} | all-to-all | bytes 262144 | tf_op jit(solution)/shard_map/all_to_all | solution.py:167
  51.4 0.1 spread.1
  51.6 15.8 %all_to_all.21 = bf16[16,32,4,128]{3,2,1,0:T(4,128)(2,1)S(1)} all-to-all(bf16[16,32,4,128]{3,2,1,0:T(4,128)(2,1)S(1)} %bitcast.19), channel_id=1, replica_groups=mesh['z'=32,'x'=4,'y'=4,'core'=2] {'x','y'}, dimensions={0} | all-to-all | bytes 1048576 | tf_op jit(solution)/shard_map/all_to_all | solution.py:189
  67.3 1.0 turn.1
  68.4 0.0 copy-start.2
  68.4 0.0 copy-start.3
  68.4 5.4 %all-gather = bf16[8,448,128]{2,1,0:T(8,128)(2,1)S(1)} all-gather(bf16[4,448,128]{2,1,0:T(8,128)(2,1)S(1)} %turn.1), channel_id=2, replica_groups=mesh['z'=32,'x'=4,'y'=4,'core'=2] {'core'}, dimensions={0}, use_global_device_ids=true | all-gather | bytes 1376256 | tf_op jit(solution)/shard_map/all_gather | solution.py:191
  73.9 0.0 copy-done
  73.9 0.0 copy-done.1
  73.9 0.0 copy-done.2
  73.9 0.0 copy-done.3
  73.9 0.6 copy-done.5
  74.5 0.0 copy-done.6
  74.5 7.8 %attend.1 = (bf16[128,512]{1,0:T(8,128)(2,1)}, bf16[128,512]{1,0:T(8,128)(2,1)}, bf16[4,8,56,128]{3,2,1,0:T(8,128)(2,1)S(1)}, bf16[4,8,56,128]{3,2,1,0:T(8,128)(2,1)S(1)}) custom-call(s32[2]{0:T(128)S(1)} %copy-done.5, s32[1,8]{1,0:T(1,128)S(1)} %copy-done.6, s32[1]{0:T(128)} %bitcast.core_ref, bf16[2,4,8,56,128]{4,3,2,1,0:T(8,128)(2,1)S(1)} %bitcast.18, ...), custom_call_target="tpu_custom_call" | custom-call | tf_op jit(solution)/shard_map/attend/pallas_call | solution.py:193
  82.4 2.3 %collective-permute-start = (bf16[4,8,56,128]{3,2,1,0:T(8,128)(2,1)S(1)}, bf16[4,8,56,128]{3,2,1,0:T(8,128)(2,1)S(1)}, u32[]{:S(2)}, u32[]{:S(2)}) collective-permute-start(bf16[4,8,56,128]{3,2,1,0:T(8,128)(2,1)S(1)} %get-tuple-element.14), channel_id=1, source_target_pairs={{0,1},{1,0},{2,3},{3,2},{4,5},{5,4},{6,7},{7,6},{8,9},{9,8},{10,11... | collective-permute-start | bytes 1376264 | tf_op jit(solution)/shard_map/ppermute | solution.py:206
  84.6 1.4 %collective-permute-done = bf16[4,8,56,128]{3,2,1,0:T(8,128)(2,1)S(1)} collective-permute-done((bf16[4,8,56,128]{3,2,1,0:T(8,128)(2,1)S(1)}, bf16[4,8,56,128]{3,2,1,0:T(8,128)(2,1)S(1)}, u32[]{:S(2)}, u32[]{:S(2)}) %collective-permute-start) | collective-permute-done | bytes 458784 | tf_op jit(solution)/shard_map/ppermute | solution.py:206
  86.1 1.5 %join.1 = bf16[4,4,32,4,128]{4,3,2,1,0:T(4,128)(2,1)S(1)} custom-call(bf16[4,448,128]{2,1,0:T(8,128)(2,1)S(1)} %bitcast.27, bf16[4,448,128]{2,1,0:T(8,128)(2,1)S(1)} %bitcast.28), custom_call_target="tpu_custom_call" | custom-call | tf_op jit(solution)/shard_map/join/pallas_call | solution.py:207
  87.5 13.3 %all_to_all.22 = bf16[16,32,4,128]{3,2,1,0:T(4,128)(2,1)S(1)} all-to-all(bf16[16,32,4,128]{3,2,1,0:T(4,128)(2,1)S(1)} %bitcast.22), channel_id=1, replica_groups=mesh['z'=32,'x'=4,'y'=4,'core'=2] {'x','y'}, dimensions={0} | all-to-all | bytes 1048576 | tf_op jit(solution)/shard_map/all_to_all | solution.py:208
  100.9 0.1 sum.1
  101.0 33.7 %all_to_all.23 = bf16[32,16,128]{2,1,0:T(8,128)(2,1)S(1)} all-to-all(bf16[32,16,128]{2,1,0:T(8,128)(2,1)S(1)} %bitcast.24), channel_id=1, replica_groups={{512,544,576,608,640,672,704,736,768,800,832,864,896,928,960,992,0,32,6..., dimensions={0} | all-to-all | bytes 262144 | tf_op jit(solution)/shard_map/all_to_all | solution.py:167
  134.7 0.9 unpack.1
  (4 shorter events, 0.0 us)
Async XLA Ops:
  0.6 0.9 copy-start.4
  68.4 5.5 %copy-start = (bf16[448,512]{1,0:T(8,128)(2,1)S(1)}, bf16[448,512]{1,0:T(8,128)(2,1)}, u32[]{:S(2)}) copy-start(bf16[448,512]{1,0:T(8,128)(2,1)} %wk_ref.1) | copy-start | bytes 1376260
  68.4 5.5 %copy-start.1 = (bf16[448,512]{1,0:T(8,128)(2,1)S(1)}, bf16[448,512]{1,0:T(8,128)(2,1)}, u32[]{:S(2)}) copy-start(bf16[448,512]{1,0:T(8,128)(2,1)} %wv_ref.1) | copy-start | bytes 1376260
  68.4 5.5 %copy-start.2 = (bf16[128,512]{1,0:T(8,128)(2,1)S(1)}, bf16[128,512]{1,0:T(8,128)(2,1)}, u32[]{:S(2)}) copy-start(bf16[128,512]{1,0:T(8,128)(2,1)} %q_ref.1) | copy-start | bytes 393220
  68.4 5.5 %copy-start.3 = (bf16[128,512]{1,0:T(8,128)(2,1)S(1)}, bf16[128,512]{1,0:T(8,128)(2,1)}, u32[]{:S(2)}) copy-start(bf16[128,512]{1,0:T(8,128)(2,1)} %g_ref.1) | copy-start | bytes 393220
  73.9 0.7 copy-start.5
  73.9 0.7 copy-start.6
  82.4 3.7 %collective-permute-start = (bf16[4,8,56,128]{3,2,1,0:T(8,128)(2,1)S(1)}, bf16[4,8,56,128]{3,2,1,0:T(8,128)(2,1)S(1)}, u32[]{:S(2)}, u32[]{:S(2)}) collective-permute-start(bf16[4,8,56,128]{3,2,1,0:T(8,128)(2,1)S(1)} %get-tuple-element.14), channel_id=1, source_target_pairs={{0,1},{1,0},{2,3},{3,2},{4,5},{5,4},{6,7},{7,6},{8,9},{9,8},{10,11... | collective-permute-start | bytes 1376264 | tf_op jit(solution)/shard_map/ppermute | solution.py:206

commit v3 on v2

v3 whole, which is shorter than its diff:
```python
import jax
import jax.numpy as jnp
from jax import lax
from jax.experimental import pallas as pl
from jax.experimental.pallas import tpu as pltpu
from jax.sharding import Mesh, PartitionSpec as P

HDIM = 128
SPAN = 64
NB_LEN = 128
MAX_NB = 4
CH_DEV = 2
SLOTS = 8
X_CHIPS = 4
CORES = 2
FIRST_IN = 24
FIRST_OUT = 16
BF = jnp.bfloat16
F32 = jnp.float32
VMEM_LIMIT = 48 * 1024 * 1024


def vmem():
    return pl.BlockSpec(memory_space=pltpu.VMEM)


def smem():
    return pl.BlockSpec(memory_space=pltpu.SMEM)


def one_hot(n_z, n_x, first):
    n = n_z * n_x
    row = lax.broadcasted_iota(jnp.int32, (n, n), 0)
    col = lax.broadcasted_iota(jnp.int32, (n, n), 1)
    place, x = lax.rem(row, n_z), lax.div(row, n_z)
    return jnp.where(col == (place ^ first) * n_x + x, 1.0, 0.0).astype(BF)


def put_pairs(out_ref, rows):
    for i in range(out_ref.shape[1]):
        out_ref[:, i, :] = jnp.concatenate([rows[2 * i], rows[2 * i + 1]], axis=1)


def get_pairs(in_ref):
    flat = in_ref.shape[2] // 2
    return [in_ref[:, x // 2, (x % 2) * flat : (x % 2 + 1) * flat] for x in range(2 * in_ref.shape[1])]


def fold(rows):
    half = rows.shape[0] // 2
    return jnp.concatenate([rows[:half], rows[half:]], axis=1)


def unfold(rows):
    flat = rows.shape[1] // 2
    return jnp.concatenate([rows[:, :flat], rows[:, flat:]], axis=0)


def pack_kernel(flat_ref, out_ref):
    n_z, n_x = out_ref.shape[0], 2 * out_ref.shape[1]
    nt = (((1,), (1,)), ((), ()))
    turned = lax.dot_general(one_hot(n_z, n_x, FIRST_IN), flat_ref[...], nt, preferred_element_type=F32).astype(BF)
    put_pairs(out_ref, [turned[x * n_z : (x + 1) * n_z] for x in range(n_x)])


def unpack_kernel(in_ref, out_ref):
    n_z, n_x = in_ref.shape[0], 2 * in_ref.shape[1]
    rows = jnp.concatenate(get_pairs(in_ref), axis=0)
    tn = (((0,), (0,)), ((), ()))
    out_ref[...] = lax.dot_general(rows, one_hot(n_z, n_x, FIRST_OUT), tn, preferred_element_type=F32).astype(BF)


def spread_kernel(in_ref, out_ref):
    for x, rows in enumerate(get_pairs(in_ref)):
        own = fold(rows)
        for y in range(out_ref.shape[1]):
            out_ref[x, y] = own


def turn_kernel(in_ref, out_ref):
    n_x, n_y = in_ref.shape[:2]
    for y in range(n_y):
        out_ref[y] = jnp.concatenate([unfold(in_ref[x, y]) for x in range(n_x)], axis=0).T


def join_kernel(core_ref, keep_ref, both_ref, out_ref):
    n_x, n_y = out_ref.shape[:2]
    n_z = 2 * out_ref.shape[2]
    other = 1 - core_ref[0]
    for y in range(n_y):
        turned = (keep_ref[y].astype(F32) + both_ref[other, y].astype(F32)).astype(BF).T
        for x in range(n_x):
            out_ref[x, y] = fold(turned[x * n_z : (x + 1) * n_z])


def sum_kernel(in_ref, out_ref):
    n_x, n_y = in_ref.shape[:2]
    first = FIRST_IN ^ FIRST_OUT
    run = first & -first if first else out_ref.shape[0]
    rows = []
    for x in range(n_x):
        total = in_ref[x, 0].astype(F32)
        for y in range(1, n_y):
            total = total + in_ref[x, y].astype(F32)
        total = unfold(total.astype(BF))
        rows.append(jnp.concatenate([total[k ^ first : (k ^ first) + run] for k in range(0, total.shape[0], run)], axis=0))
    put_pairs(out_ref, rows)


def attend_kernel(
    counts_ref, slots_ref, core_ref, rows_ref, wk_ref, wv_ref, q_ref, g_ref, att_ref, dq_ref, keep_ref, send_ref, x_ref, dk_ref, dv_ref, part_ref
):
    n_core, n_y, _, chunk, _ = rows_ref.shape
    heads = q_ref.shape[1] // HDIM
    span_rows = MAX_NB * NB_LEN
    factor = 1.0 / HDIM**0.5
    for j in range(SLOTS):
        slot = slots_ref[0, j]
        for b in range(n_core * n_y):
            x_ref[b * chunk : (b + 1) * chunk, j * NB_LEN : (j + 1) * NB_LEN] = rows_ref[b % n_core, b // n_core, slot]
    col = lax.broadcasted_iota(jnp.int32, (1, span_rows), 1)
    bias = [jnp.where(col < counts_ref[c] * NB_LEN, 0.0, -jnp.inf) for c in range(CH_DEV)]
    nt = (((1,), (1,)), ((), ()))
    tn = (((0,), (0,)), ((), ()))
    toks = [slice(c * SPAN, (c + 1) * SPAN) for c in range(CH_DEV)]
    owns = [slice(c * span_rows, (c + 1) * span_rows) for c in range(CH_DEV)]

    def project(h):
        cols = slice(h * HDIM, (h + 1) * HDIM)
        key = lax.dot_general(wk_ref[:, cols], x_ref[...], tn, preferred_element_type=F32)
        value = lax.dot_general(wv_ref[:, cols], x_ref[...], tn, preferred_element_type=F32).astype(BF)
        key_hi = key.astype(BF)
        key_lo = (key - key_hi.astype(F32)).astype(BF)
        return jnp.concatenate([key_hi, key_lo], axis=0), value

    def score(h, c, key_two, value):
        cols = slice(h * HDIM, (h + 1) * HDIM)
        query = q_ref[toks[c], cols]
        scores = jnp.dot(jnp.concatenate([query, query], axis=1), key_two[:, owns[c]], preferred_element_type=F32)
        dprobs = jnp.dot(g_ref[toks[c], cols], value[:, owns[c]], preferred_element_type=F32)
        return scores, dprobs

    def soften(c, scores, dprobs):
        scores = scores * factor + bias[c]
        top = jnp.max(scores, axis=1, keepdims=True)
        expo = jnp.exp(scores - top)
        probs = expo * (1.0 / jnp.sum(expo, axis=1, keepdims=True))
        inner = jnp.sum(probs * dprobs, axis=1, keepdims=True)
        return probs.astype(BF), (probs * (dprobs - inner)).astype(BF)

    def finish(h, c, key_two, value, probs_b, dscores):
        cols = slice(h * HDIM, (h + 1) * HDIM)
        query, grad = q_ref[toks[c], cols], g_ref[toks[c], cols]
        att = lax.dot_general(probs_b, value[:, owns[c]], nt, preferred_element_type=F32)
        att_ref[toks[c], cols] = att.astype(BF)
        dq = lax.dot_general(dscores, key_two[:, owns[c]], nt, preferred_element_type=F32)
        dq_ref[toks[c], cols] = ((dq[:, :HDIM] + dq[:, HDIM:]) * factor).astype(BF)
        dk_ref[cols, owns[c]] = (lax.dot_general(query, dscores, tn, preferred_element_type=F32) * factor).astype(BF)
        dv_ref[cols, owns[c]] = lax.dot_general(grad, probs_b, tn, preferred_element_type=F32).astype(BF)

    pairs = [(h, c) for h in range(heads) for c in range(CH_DEV)]
    kv, raw, soft = {0: project(0)}, {}, {}
    for i in range(len(pairs) + 2):
        if i < len(pairs):
            h, c = pairs[i]
            raw[i] = score(h, c, *kv[h])
        if c == 0 and i < len(pairs) and h + 1 < heads:
            kv[h + 1] = project(h + 1)
        if 1 <= i <= len(pairs):
            soft[i - 1] = soften(pairs[i - 1][1], *raw.pop(i - 1))
        if i >= 2:
            ph, pc = pairs[i - 2]
            finish(ph, pc, *kv[ph], *soft.pop(i - 2))
    part = jnp.dot(wk_ref[...], dk_ref[...], preferred_element_type=F32)
    part = (part + jnp.dot(wv_ref[...], dv_ref[...], preferred_element_type=F32)).astype(BF)
    for b in range(n_core * n_y):
        part_ref[b] = part[b * chunk : (b + 1) * chunk]
    core = core_ref[0]
    for j in range(SLOTS):
        slot = slots_ref[0, j]
        for y in range(n_y):
            keep_ref[y, slot] = part_ref[y * n_core + core, :, j * NB_LEN : (j + 1) * NB_LEN]
            send_ref[y, slot] = part_ref[y * n_core + 1 - core, :, j * NB_LEN : (j + 1) * NB_LEN]


def call(kernel, outs, n_in, name, small=0, scratch=()):
    one = isinstance(outs, jax.ShapeDtypeStruct)
    return pl.pallas_call(
        kernel,
        out_shape=outs,
        in_specs=[smem()] * small + [vmem()] * n_in,
        out_specs=vmem() if one else tuple(vmem() for _ in outs),
        scratch_shapes=scratch,
        compiler_params=pltpu.CompilerParams(vmem_limit_bytes=VMEM_LIMIT),
        name=name,
    )


def exchange(messages, first):
    n_z = messages.shape[0]
    return lax.all_to_all(
        messages, "z", split_axis=0, concat_axis=0, axis_index_groups=[[k ^ first for k in range(n_z)]], tiled=True
    )


def per_device(queries, neighbours, key_weight, value_weight, counts, slot_map, d_attended):
    n_z, n_x, n_y, n_core = (lax.axis_size(a) for a in ("z", "x", "y", "core"))
    n_seq = n_z * n_x
    chunk = neighbours.shape[3]
    enc, width = key_weight.shape
    flat = SLOTS * chunk
    rows = SLOTS * NB_LEN

    def shape(*dims):
        return jax.ShapeDtypeStruct(dims, BF)

    pairs = shape(n_z, n_x // 2, 2 * flat)
    folded = shape(n_x, n_y, n_z // 2, 2 * flat)
    merged = (n_x * n_y, n_z // 2, 2 * flat)
    turned = neighbours.transpose(1, 2, 3, 0).reshape(flat, n_seq)
    core, turned = lax.optimization_barrier((lax.axis_index("core").reshape(1), turned))
    out = call(pack_kernel, pairs, 1, "pack")(turned)
    out = exchange(out, FIRST_IN)
    out = call(spread_kernel, folded, 1, "spread")(out)
    out = lax.all_to_all(out.reshape(merged), ("x", "y"), split_axis=0, concat_axis=0, tiled=True)
    out = call(turn_kernel, shape(n_y, flat, NB_LEN), 1, "turn")(out.reshape(folded.shape))
    out = lax.all_gather(out, "core", axis=0).reshape(n_core, n_y, SLOTS, chunk, NB_LEN)
    half = shape(n_y, SLOTS, chunk, NB_LEN)
    attended, d_queries, keep, send = call(
        attend_kernel,
        (shape(*queries.shape), shape(*queries.shape), half, half),
        5,
        "attend",
        small=3,
        scratch=(
            pltpu.VMEM((enc, rows), BF),
            pltpu.VMEM((width, rows), BF),
            pltpu.VMEM((width, rows), BF),
            pltpu.VMEM((n_core * n_y, chunk, rows), BF),
        ),
    )(counts, slot_map, core, out, key_weight, value_weight, queries, d_attended)
    both = lax.all_gather(send.reshape(n_y, flat, NB_LEN), "core", axis=0)
    back = call(join_kernel, folded, 2, "join", small=1)(core, keep.reshape(n_y, flat, NB_LEN), both)
    back = lax.all_to_all(back.reshape(merged), ("x", "y"), split_axis=0, concat_axis=0, tiled=True)
    back = call(sum_kernel, pairs, 1, "sum")(back.reshape(folded.shape))
    home = exchange(back, FIRST_OUT)
    grad = call(unpack_kernel, shape(flat, n_seq), 1, "unpack")(home)
    d_neighbours = grad.reshape(1, SLOTS, chunk, n_seq).transpose(3, 0, 1, 2)
    return (attended, d_queries, d_neighbours)


def solution(mesh):
    n_seq, n_head = mesh.devices.shape
    fine = Mesh(mesh.devices.reshape(n_seq // X_CHIPS, X_CHIPS, n_head // CORES, CORES), ("z", "x", "y", "core"))
    seq, head = ("z", "x"), ("y", "core")
    in_specs = (
        P(seq, head),
        P(None, seq, None, head),
        P(None, head),
        P(None, head),
        P(seq),
        P(seq, None),
        P(seq, head),
    )
    out_specs = (P(seq, head), P(seq, head), P(None, seq, None, head))
    return jax.shard_map(
        per_device, mesh=fine, in_specs=in_specs, out_specs=out_specs, check_vma=False
    )
```

time: 136 us -> 127 us (0.934)
  Pallas kernels: 11.9 us -> 8.28 us
  starting transfers between devices: 2.27 us -> 0 us
  blocking collectives: 118 us -> 116 us
  waiting for transfers between devices: 1.42 us -> 0 us
    all_to_all x2, blocking collectives: 83.2 us -> 79.6 us  [exchange(): lax.all_to_all(messages, 'z', split_axis=0, concat_axis=0, axis_index_gro...]
    all_gather x0 -> x1, blocking collectives: none -> 2.46 us  [per_device(): both = lax.all_gather(send.reshape(n_y, flat, NB_LEN), 'core', axis=0)]
    ppermute x1 -> x0, starting transfers between devices: 2.27 us -> none  [per_device(): got = lax.ppermute(send, 'core', [(0, 1), (1, 0)])]
    pallas_call x1, Pallas kernels: 7.83 us -> 5.79 us  [per_device(): call(attend_kernel, (shape(*queries.shape), shape(*queries.shape), half,...]
    ppermute x1 -> x0, waiting for transfers between devices: 1.42 us -> none  [per_device(): got = lax.ppermute(send, 'core', [(0, 1), (1, 0)])]
  transfers between devices with their start and end apart: 1 -> 0, of which waited for: 1 -> 0; matrix products, arithmetic and copies ran while one was open for 0% -> 0% of each run, Pallas kernels for 0% -> 0%
where the time goes in v3:
time: 127 us; the launch traced here: 126 us
  blocking collectives  116 us (91%)
  Pallas kernels  8.28 us (7%)
  local copies, waits for them, and re-layouts  1.56 us (1%)
    all_to_all x2, blocking collectives, exchange(): lax.all_to_all(messages, 'z', split_axis=0, concat_axis=0, axis_index_gro...  79.6 us
    all_to_all x1, blocking collectives, per_device(): lax.all_to_all(out.reshape(merged), ('x', 'y'), split_axis=0, concat_axis...  15.4 us
    all_to_all x1, blocking collectives, per_device(): lax.all_to_all(back.reshape(merged), ('x', 'y'), split_axis=0, concat_axi...  12.8 us
    pallas_call x1, Pallas kernels, per_device(): call(attend_kernel, (shape(*queries.shape), shape(*queries.shape), half,...  5.79 us
    all_gather x1, blocking collectives, per_device(): lax.all_gather(out, 'core', axis=0)  5.39 us

profile of v3, /device:TPU:1, one launch (start us, length us, event | category | flops | bytes accessed | tf_op | source)
XLA Modules:
  0.0 126.2 jit_solution(4667900356581194507)
XLA Ops:
  0.6 0.0 copy-start.4
  0.6 0.9 copy-done.4
  1.5 0.3 pack.1
  1.8 47.8 %all_to_all.20.in_ref = bf16[32,2,896]{2,1,0:T(2,128)(2,1)S(1)} all-to-all(bf16[32,2,896]{2,1,0:T(2,128)(2,1)S(1)} %pack.1), channel_id=1, replica_groups={{768,800,832,864,896,928,960,992,512,544,576,608,640,672,704,736,256,28..., dimensions={0} | all-to-all | bytes 229376 | tf_op jit(solution)/shard_map/all_to_all | solution.py:201
  49.6 0.2 spread.1
  49.9 15.4 %all_to_all.21 = bf16[16,16,896]{2,1,0:T(8,128)(2,1)S(1)} all-to-all(bf16[16,16,896]{2,1,0:T(8,128)(2,1)S(1)} %bitcast.16), channel_id=1, replica_groups=mesh['z'=32,'x'=4,'y'=4,'core'=2] {'x','y'}, dimensions={0} | all-to-all | bytes 917504 | tf_op jit(solution)/shard_map/all_to_all | solution.py:225
  65.3 0.4 turn.1
  65.7 0.0 copy-start
  65.7 0.0 copy-start.1
  65.7 0.0 copy-start.2
  65.7 0.0 copy-start.3
  65.7 5.4 %all-gather = bf16[8,448,128]{2,1,0:T(8,128)(2,1)S(1)} all-gather(bf16[4,448,128]{2,1,0:T(8,128)(2,1)S(1)} %turn.1), channel_id=2, replica_groups=mesh['z'=32,'x'=4,'y'=4,'core'=2] {'core'}, dimensions={0}, use_global_device_ids=true | all-gather | bytes 1376256 | tf_op jit(solution)/shard_map/all_gather | solution.py:227
  71.1 0.0 copy-done
  71.1 0.0 copy-done.1
  71.1 0.0 copy-done.2
  71.2 0.6 copy-done.5
  71.8 0.0 copy-done.6
  71.8 5.8 %attend.1 = (bf16[128,512]{1,0:T(8,128)(2,1)}, bf16[128,512]{1,0:T(8,128)(2,1)}, bf16[4,8,56,128]{3,2,1,0:T(8,128)(2,1)S(1)}, bf16[4,8,56,128]{3,2,1,0:T(8,128)(2,1)S(1)}) custom-call(s32[2]{0:T(128)S(1)} %copy-done.5, s32[1,8]{1,0:T(1,128)S(1)} %copy-done.6, s32[1]{0:T(128)} %bitcast.core_ref, bf16[2,4,8,56,128]{4,3,2,1,0:T(8,128)(2,1)S(1)} %bitcast.14, ...), custom_call_target="tpu_custom_call" | custom-call | tf_op jit(solution)/shard_map/attend/pallas_call | solution.py:229
  77.6 2.5 %all_gather.11.both_ref = bf16[2,4,448,128]{3,2,1,0:T(8,128)(2,1)S(1)} all-gather(bf16[1,4,448,128]{3,2,1,0:T(8,128)(2,1)S(1)} %bitcast.20), channel_id=1, replica_groups=mesh['z'=32,'x'=4,'y'=4,'core'=2] {'core'}, dimensions={0}, use_global_device_ids=true | all-gather | bytes 1376256 | tf_op jit(solution)/shard_map/all_gather | solution.py:242
  80.0 0.3 join.1
  80.3 12.8 %all_to_all.22 = bf16[16,16,896]{2,1,0:T(8,128)(2,1)S(1)} all-to-all(bf16[16,16,896]{2,1,0:T(8,128)(2,1)S(1)} %bitcast.18), channel_id=1, replica_groups=mesh['z'=32,'x'=4,'y'=4,'core'=2] {'x','y'}, dimensions={0} | all-to-all | bytes 917504 | tf_op jit(solution)/shard_map/all_to_all | solution.py:244
  93.1 0.2 sum.1
  93.3 31.8 %all_to_all.23.in_ref = bf16[32,2,896]{2,1,0:T(2,128)(2,1)S(1)} all-to-all(bf16[32,2,896]{2,1,0:T(2,128)(2,1)S(1)} %sum.1), channel_id=1, replica_groups={{512,544,576,608,640,672,704,736,768,800,832,864,896,928,960,992,0,32,6..., dimensions={0} | all-to-all | bytes 229376 | tf_op jit(solution)/shard_map/all_to_all | solution.py:201
  125.1 1.1 unpack.1
  (3 shorter events, 0.0 us)
Async XLA Ops:
  0.6 0.9 copy-start.4
  65.7 5.4 %copy-start = (bf16[448,512]{1,0:T(8,128)(2,1)S(1)}, bf16[448,512]{1,0:T(8,128)(2,1)}, u32[]{:S(2)}) copy-start(bf16[448,512]{1,0:T(8,128)(2,1)} %wk_ref.1) | copy-start | bytes 1376260
  65.7 5.4 %copy-start.1 = (bf16[448,512]{1,0:T(8,128)(2,1)S(1)}, bf16[448,512]{1,0:T(8,128)(2,1)}, u32[]{:S(2)}) copy-start(bf16[448,512]{1,0:T(8,128)(2,1)} %wv_ref.1) | copy-start | bytes 1376260
  65.7 5.4 %copy-start.2 = (bf16[128,512]{1,0:T(8,128)(2,1)S(1)}, bf16[128,512]{1,0:T(8,128)(2,1)}, u32[]{:S(2)}) copy-start(bf16[128,512]{1,0:T(8,128)(2,1)} %q_ref.1) | copy-start | bytes 393220
  65.7 5.4 %copy-start.3 = (bf16[128,512]{1,0:T(8,128)(2,1)S(1)}, bf16[128,512]{1,0:T(8,128)(2,1)}, u32[]{:S(2)}) copy-start(bf16[128,512]{1,0:T(8,128)(2,1)} %g_ref.1) | copy-start | bytes 393220
  71.1 0.7 copy-start.5
  71.1 0.7 copy-start.6

commit v4 on v3

--- a/solution.py
+++ b/solution.py
@@ -15,6 +15,8 @@
 CORES = 2
 FIRST_IN = 24
 FIRST_OUT = 16
+FIRST_X = 2
+FIRST_Y = 2
 BF = jnp.bfloat16
 F32 = jnp.float32
 VMEM_LIMIT = 48 * 1024 * 1024
@@ -63,24 +65,29 @@
     put_pairs(out_ref, [turned[x * n_z : (x + 1) * n_z] for x in range(n_x)])
 
 
-def unpack_kernel(in_ref, out_ref):
+def unpack_kernel(in_ref, att_ref, dq_ref, out_ref, att_out, dq_out, sem):
+    copies = [pltpu.make_async_copy(att_ref, att_out, sem.at[0]), pltpu.make_async_copy(dq_ref, dq_out, sem.at[1])]
+    for copy in copies:
+        copy.start()
     n_z, n_x = in_ref.shape[0], 2 * in_ref.shape[1]
     rows = jnp.concatenate(get_pairs(in_ref), axis=0)
     tn = (((0,), (0,)), ((), ()))
     out_ref[...] = lax.dot_general(rows, one_hot(n_z, n_x, FIRST_OUT), tn, preferred_element_type=F32).astype(BF)
+    for copy in copies:
+        copy.wait()
 
 
 def spread_kernel(in_ref, out_ref):
     for x, rows in enumerate(get_pairs(in_ref)):
         own = fold(rows)
         for y in range(out_ref.shape[1]):
-            out_ref[x, y] = own
+            out_ref[x ^ FIRST_X, y] = own
 
 
 def turn_kernel(in_ref, out_ref):
     n_x, n_y = in_ref.shape[:2]
     for y in range(n_y):
-        out_ref[y] = jnp.concatenate([unfold(in_ref[x, y]) for x in range(n_x)], axis=0).T
+        out_ref[y ^ FIRST_Y] = jnp.concatenate([unfold(in_ref[x, y]) for x in range(n_x)], axis=0).T
 
 
 def join_kernel(core_ref, keep_ref, both_ref, out_ref):
@@ -90,7 +97,7 @@
     for y in range(n_y):
         turned = (keep_ref[y].astype(F32) + both_ref[other, y].astype(F32)).astype(BF).T
         for x in range(n_x):
-            out_ref[x, y] = fold(turned[x * n_z : (x + 1) * n_z])
+            out_ref[x, y ^ FIRST_Y] = fold(turned[x * n_z : (x + 1) * n_z])
 
 
 def sum_kernel(in_ref, out_ref):
@@ -99,9 +106,9 @@
     run = first & -first if first else out_ref.shape[0]
     rows = []
     for x in range(n_x):
-        total = in_ref[x, 0].astype(F32)
+        total = in_ref[x ^ FIRST_X, 0].astype(F32)
         for y in range(1, n_y):
-            total = total + in_ref[x, y].astype(F32)
+            total = total + in_ref[x ^ FIRST_X, y].astype(F32)
         total = unfold(total.astype(BF))
         rows.append(jnp.concatenate([total[k ^ first : (k ^ first) + run] for k in range(0, total.shape[0], run)], axis=0))
     put_pairs(out_ref, rows)
@@ -183,13 +190,13 @@
             send_ref[y, slot] = part_ref[y * n_core + 1 - core, :, j * NB_LEN : (j + 1) * NB_LEN]
 
 
-def call(kernel, outs, n_in, name, small=0, scratch=()):
+def call(kernel, outs, n_in, name, small=0, scratch=(), left=0):
     one = isinstance(outs, jax.ShapeDtypeStruct)
     return pl.pallas_call(
         kernel,
         out_shape=outs,
         in_specs=[smem()] * small + [vmem()] * n_in,
-        out_specs=vmem() if one else tuple(vmem() for _ in outs),
+        out_specs=vmem() if one else (vmem(),) * (len(outs) - left) + (pl.BlockSpec(memory_space=pl.ANY),) * left,
         scratch_shapes=scratch,
         compiler_params=pltpu.CompilerParams(vmem_limit_bytes=VMEM_LIMIT),
         name=name,
@@ -201,6 +208,12 @@
     return lax.all_to_all(
         messages, "z", split_axis=0, concat_axis=0, axis_index_groups=[[k ^ first for k in range(n_z)]], tiled=True
     )
+
+
+def exchange_xy(messages, n_y):
+    first = FIRST_X * n_y + FIRST_Y
+    places = [[k ^ first for k in range(messages.shape[0])]]
+    return lax.all_to_all(messages, ("x", "y"), split_axis=0, concat_axis=0, axis_index_groups=places, tiled=True)
 
 
 def per_device(queries, neighbours, key_weight, value_weight, counts, slot_map, d_attended):
@@ -222,7 +235,7 @@
     out = call(pack_kernel, pairs, 1, "pack")(turned)
     out = exchange(out, FIRST_IN)
     out = call(spread_kernel, folded, 1, "spread")(out)
-    out = lax.all_to_all(out.reshape(merged), ("x", "y"), split_axis=0, concat_axis=0, tiled=True)
+    out = exchange_xy(out.reshape(merged), n_y)
     out = call(turn_kernel, shape(n_y, flat, NB_LEN), 1, "turn")(out.reshape(folded.shape))
     out = lax.all_gather(out, "core", axis=0).reshape(n_core, n_y, SLOTS, chunk, NB_LEN)
     half = shape(n_y, SLOTS, chunk, NB_LEN)
@@ -241,10 +254,17 @@
     )(counts, slot_map, core, out, key_weight, value_weight, queries, d_attended)
     both = lax.all_gather(send.reshape(n_y, flat, NB_LEN), "core", axis=0)
     back = call(join_kernel, folded, 2, "join", small=1)(core, keep.reshape(n_y, flat, NB_LEN), both)
-    back = lax.all_to_all(back.reshape(merged), ("x", "y"), split_axis=0, concat_axis=0, tiled=True)
+    back = exchange_xy(back.reshape(merged), n_y)
     back = call(sum_kernel, pairs, 1, "sum")(back.reshape(folded.shape))
     home = exchange(back, FIRST_OUT)
-    grad = call(unpack_kernel, shape(flat, n_seq), 1, "unpack")(home)
+    grad, attended, d_queries = call(
+        unpack_kernel,
+        (shape(flat, n_seq), shape(*queries.shape), shape(*queries.shape)),
+        3,
+        "unpack",
+        scratch=(pltpu.SemaphoreType.DMA((2,)),),
+        left=2,
+    )(home, attended, d_queries)
     d_neighbours = grad.reshape(1, SLOTS, chunk, n_seq).transpose(3, 0, 1, 2)
     return (attended, d_queries, d_neighbours)
 

time: 127 us -> 123 us (0.969)
  blocking collectives: 116 us -> 112 us
    all_to_all x2, blocking collectives: 28.2 us -> 24.2 us  [exchange_xy(): lax.all_to_all(messages, ('x', 'y'), split_axis=0, concat_axis=0, axis_in...]
where the time goes in v4:
time: 123 us; the launch traced here: 122 us
  blocking collectives  112 us (91%)
  Pallas kernels  7.84 us (6%)
  local copies, waits for them, and re-layouts  1.56 us (1%)
    all_to_all x2, blocking collectives, exchange(): lax.all_to_all(messages, 'z', split_axis=0, concat_axis=0, axis_index_gro...  79.4 us
    all_to_all x2, blocking collectives, exchange_xy(): lax.all_to_all(messages, ('x', 'y'), split_axis=0, concat_axis=0, axis_in...  24.2 us
    all_gather x1, blocking collectives, per_device(): lax.all_gather(out, 'core', axis=0)  5.58 us
    pallas_call x1, Pallas kernels, per_device(): call(attend_kernel, (shape(*queries.shape), shape(*queries.shape), half,...  5.1 us
    all_gather x1, blocking collectives, per_device(): both = lax.all_gather(send.reshape(n_y, flat, NB_LEN), 'core', axis=0)  2.48 us

profile of v4, /device:TPU:1, one launch (start us, length us, event | category | flops | bytes accessed | tf_op | source)
XLA Modules:
  0.0 121.8 jit_solution(9262251070508183209)
XLA Ops:
  0.6 0.0 copy-start.4
  0.6 0.9 copy-done.4
  1.5 0.3 pack.1
  1.8 47.8 %all_to_all.20.in_ref = bf16[32,2,896]{2,1,0:T(2,128)(2,1)S(1)} all-to-all(bf16[32,2,896]{2,1,0:T(2,128)(2,1)S(1)} %pack.1), channel_id=1, replica_groups={{768,800,832,864,896,928,960,992,512,544,576,608,640,672,704,736,256,28..., dimensions={0} | all-to-all | bytes 229376 | tf_op jit(solution)/shard_map/all_to_all | solution.py:208
  49.6 0.2 spread.1
  49.9 12.3 %all_to_all.21 = bf16[16,16,896]{2,1,0:T(8,128)(2,1)S(1)} all-to-all(bf16[16,16,896]{2,1,0:T(8,128)(2,1)S(1)} %bitcast.16), channel_id=1, replica_groups={{20,22,16,18,28,30,24,26,4,6,0,2,12,14,8,10},{21,23,17,19,29,31,25,27,5..., dimensions={0} | all-to-all | bytes 917504 | tf_op jit(solution)/shard_map/all_to_all | solution.py:216
  62.1 0.4 turn.1
  62.5 0.0 copy-start
  62.5 0.0 copy-start.1
  62.6 0.0 copy-start.2
  62.6 0.0 copy-start.3
  62.6 5.6 %all-gather = bf16[8,448,128]{2,1,0:T(8,128)(2,1)S(1)} all-gather(bf16[4,448,128]{2,1,0:T(8,128)(2,1)S(1)} %turn.1), channel_id=2, replica_groups=mesh['z'=32,'x'=4,'y'=4,'core'=2] {'core'}, dimensions={0}, use_global_device_ids=true | all-gather | bytes 1376256 | tf_op jit(solution)/shard_map/all_gather | solution.py:240
  68.2 0.0 copy-done
  68.2 0.0 copy-done.2
  68.2 0.0 copy-done.3
  68.2 0.6 copy-done.5
  68.8 0.0 copy-done.6
  68.8 5.1 %attend.1 = (bf16[128,512]{1,0:T(8,128)(2,1)S(1)}, bf16[128,512]{1,0:T(8,128)(2,1)S(1)}, bf16[4,8,56,128]{3,2,1,0:T(8,128)(2,1)S(1)}, bf16[4,8,56,128]{3,2,1,0:T(8,128)(2,1)S(1)}) custom-call(s32[2]{0:T(128)S(1)} %copy-done.5, s32[1,8]{1,0:T(1,128)S(1)} %copy-done.6, s32[1]{0:T(128)} %bitcast.core_ref, bf16[2,4,8,56,128]{4,3,2,1,0:T(8,128)(2,1)S(1)} %bitcast.14, ...), custom_call_target="tpu_custom_call" | custom-call | tf_op jit(solution)/shard_map/attend/pallas_call | solution.py:242
  73.9 2.5 %all_gather.11.both_ref = bf16[2,4,448,128]{3,2,1,0:T(8,128)(2,1)S(1)} all-gather(bf16[1,4,448,128]{3,2,1,0:T(8,128)(2,1)S(1)} %bitcast.20), channel_id=1, replica_groups=mesh['z'=32,'x'=4,'y'=4,'core'=2] {'core'}, dimensions={0}, use_global_device_ids=true | all-gather | bytes 1376256 | tf_op jit(solution)/shard_map/all_gather | solution.py:255
  76.4 0.3 join.1
  76.7 11.9 %all_to_all.22 = bf16[16,16,896]{2,1,0:T(8,128)(2,1)S(1)} all-to-all(bf16[16,16,896]{2,1,0:T(8,128)(2,1)S(1)} %bitcast.18), channel_id=1, replica_groups={{20,22,16,18,28,30,24,26,4,6,0,2,12,14,8,10},{21,23,17,19,29,31,25,27,5..., dimensions={0} | all-to-all | bytes 917504 | tf_op jit(solution)/shard_map/all_to_all | solution.py:216
  88.6 0.2 sum.1
  88.8 31.6 %all_to_all.23.in_ref = bf16[32,2,896]{2,1,0:T(2,128)(2,1)S(1)} all-to-all(bf16[32,2,896]{2,1,0:T(2,128)(2,1)S(1)} %sum.1), channel_id=1, replica_groups={{512,544,576,608,640,672,704,736,768,800,832,864,896,928,960,992,0,32,6..., dimensions={0} | all-to-all | bytes 229376 | tf_op jit(solution)/shard_map/all_to_all | solution.py:208
  120.4 1.4 %unpack.1 = (bf16[448,128]{1,0:T(8,128)(2,1)}, bf16[128,512]{1,0:T(8,128)(2,1)}, bf16[128,512]{1,0:T(8,128)(2,1)}) custom-call(bf16[32,2,896]{2,1,0:T(2,128)(2,1)S(1)} %all_to_all.23.in_ref, bf16[128,512]{1,0:T(8,128)(2,1)S(1)} %get-tuple-element.16.att_ref, bf16[128,512]{1,0:T(8,128)(2,1)S(1)} %get-tuple-element.17.dq_ref), custom_call_target="tpu_custom_call" | custom-call | tf_op jit(solution)/shard_map/unpack/pallas_call | solution.py:260
  (3 shorter events, 0.0 us)
Async XLA Ops:
  0.6 0.9 copy-start.4
  62.5 5.6 %copy-start = (bf16[448,512]{1,0:T(8,128)(2,1)S(1)}, bf16[448,512]{1,0:T(8,128)(2,1)}, u32[]{:S(2)}) copy-start(bf16[448,512]{1,0:T(8,128)(2,1)} %wk_ref.1) | copy-start | bytes 1376260
  62.5 5.6 %copy-start.1 = (bf16[448,512]{1,0:T(8,128)(2,1)S(1)}, bf16[448,512]{1,0:T(8,128)(2,1)}, u32[]{:S(2)}) copy-start(bf16[448,512]{1,0:T(8,128)(2,1)} %wv_ref.1) | copy-start | bytes 1376260
  62.6 5.6 %copy-start.2 = (bf16[128,512]{1,0:T(8,128)(2,1)S(1)}, bf16[128,512]{1,0:T(8,128)(2,1)}, u32[]{:S(2)}) copy-start(bf16[128,512]{1,0:T(8,128)(2,1)} %q_ref.1) | copy-start | bytes 393220
  62.6 5.6 %copy-start.3 = (bf16[128,512]{1,0:T(8,128)(2,1)S(1)}, bf16[128,512]{1,0:T(8,128)(2,1)}, u32[]{:S(2)}) copy-start(bf16[128,512]{1,0:T(8,128)(2,1)} %g_ref.1) | copy-start | bytes 393220
  68.2 0.7 copy-start.5
  68.2 0.7 copy-start.6

commit v5 on v4

--- a/solution.py
+++ b/solution.py
@@ -13,7 +13,7 @@
 SLOTS = 8
 X_CHIPS = 4
 CORES = 2
-FIRST_IN = 24
+FIRST_IN = 20
 FIRST_OUT = 16
 FIRST_X = 2
 FIRST_Y = 2

time: 123 us -> 121 us (0.984)
  blocking collectives: 112 us -> 110 us
    all_to_all x2, blocking collectives: 79.4 us -> 77.7 us  [exchange(): lax.all_to_all(messages, 'z', split_axis=0, concat_axis=0, axis_index_gro...]
where the time goes in v5:
time: 121 us; the launch traced here: 120 us
  blocking collectives  110 us (91%)
  Pallas kernels  7.84 us (6%)
  local copies, waits for them, and re-layouts  1.56 us (1%)
    all_to_all x2, blocking collectives, exchange(): lax.all_to_all(messages, 'z', split_axis=0, concat_axis=0, axis_index_gro...  77.7 us
    all_to_all x2, blocking collectives, exchange_xy(): lax.all_to_all(messages, ('x', 'y'), split_axis=0, concat_axis=0, axis_in...  24.6 us
    pallas_call x1, Pallas kernels, per_device(): call(attend_kernel, (shape(*queries.shape), shape(*queries.shape), half,...  5.09 us
    all_gather x1, blocking collectives, per_device(): lax.all_gather(out, 'core', axis=0)  4.91 us
    all_gather x1, blocking collectives, per_device(): both = lax.all_gather(send.reshape(n_y, flat, NB_LEN), 'core', axis=0)  2.47 us

profile of v5, /device:TPU:1, one launch (start us, length us, event | category | flops | bytes accessed | tf_op | source)
XLA Modules:
  0.0 119.8 jit_solution(15257663823240037434)
XLA Ops:
  0.6 0.0 copy-start.4
  0.6 0.9 copy-done.4
  1.5 0.3 pack.1
  1.8 46.3 %all_to_all.20.in_ref = bf16[32,2,896]{2,1,0:T(2,128)(2,1)S(1)} all-to-all(bf16[32,2,896]{2,1,0:T(2,128)(2,1)S(1)} %pack.1), channel_id=1, replica_groups={{640,672,704,736,512,544,576,608,896,928,960,992,768,800,832,864,128,16..., dimensions={0} | all-to-all | bytes 229376 | tf_op jit(solution)/shard_map/all_to_all | solution.py:208
  48.1 0.2 spread.1
  48.4 12.7 %all_to_all.21 = bf16[16,16,896]{2,1,0:T(8,128)(2,1)S(1)} all-to-all(bf16[16,16,896]{2,1,0:T(8,128)(2,1)S(1)} %bitcast.16), channel_id=1, replica_groups={{20,22,16,18,28,30,24,26,4,6,0,2,12,14,8,10},{21,23,17,19,29,31,25,27,5..., dimensions={0} | all-to-all | bytes 917504 | tf_op jit(solution)/shard_map/all_to_all | solution.py:216
  61.1 0.4 turn.1
  61.5 0.0 copy-start
  61.5 0.0 copy-start.1
  61.5 0.0 copy-start.2
  61.6 0.0 copy-start.3
  61.6 4.9 %all-gather = bf16[8,448,128]{2,1,0:T(8,128)(2,1)S(1)} all-gather(bf16[4,448,128]{2,1,0:T(8,128)(2,1)S(1)} %turn.1), channel_id=2, replica_groups=mesh['z'=32,'x'=4,'y'=4,'core'=2] {'core'}, dimensions={0}, use_global_device_ids=true | all-gather | bytes 1376256 | tf_op jit(solution)/shard_map/all_gather | solution.py:240
  66.5 0.0 copy-done
  66.5 0.0 copy-done.1
  66.5 0.0 copy-done.2
  66.5 0.6 copy-done.5
  67.1 0.0 copy-done.6
  67.1 5.1 %attend.1 = (bf16[128,512]{1,0:T(8,128)(2,1)S(1)}, bf16[128,512]{1,0:T(8,128)(2,1)S(1)}, bf16[4,8,56,128]{3,2,1,0:T(8,128)(2,1)S(1)}, bf16[4,8,56,128]{3,2,1,0:T(8,128)(2,1)S(1)}) custom-call(s32[2]{0:T(128)S(1)} %copy-done.5, s32[1,8]{1,0:T(1,128)S(1)} %copy-done.6, s32[1]{0:T(128)} %bitcast.core_ref, bf16[2,4,8,56,128]{4,3,2,1,0:T(8,128)(2,1)S(1)} %bitcast.14, ...), custom_call_target="tpu_custom_call" | custom-call | tf_op jit(solution)/shard_map/attend/pallas_call | solution.py:242
  72.2 2.5 %all_gather.11.both_ref = bf16[2,4,448,128]{3,2,1,0:T(8,128)(2,1)S(1)} all-gather(bf16[1,4,448,128]{3,2,1,0:T(8,128)(2,1)S(1)} %bitcast.20), channel_id=1, replica_groups=mesh['z'=32,'x'=4,'y'=4,'core'=2] {'core'}, dimensions={0}, use_global_device_ids=true | all-gather | bytes 1376256 | tf_op jit(solution)/shard_map/all_gather | solution.py:255
  74.7 0.3 join.1
  75.0 11.9 %all_to_all.22 = bf16[16,16,896]{2,1,0:T(8,128)(2,1)S(1)} all-to-all(bf16[16,16,896]{2,1,0:T(8,128)(2,1)S(1)} %bitcast.18), channel_id=1, replica_groups={{20,22,16,18,28,30,24,26,4,6,0,2,12,14,8,10},{21,23,17,19,29,31,25,27,5..., dimensions={0} | all-to-all | bytes 917504 | tf_op jit(solution)/shard_map/all_to_all | solution.py:216
  86.9 0.2 sum.1
  87.1 31.4 %all_to_all.23.in_ref = bf16[32,2,896]{2,1,0:T(2,128)(2,1)S(1)} all-to-all(bf16[32,2,896]{2,1,0:T(2,128)(2,1)S(1)} %sum.1), channel_id=1, replica_groups={{512,544,576,608,640,672,704,736,768,800,832,864,896,928,960,992,0,32,6..., dimensions={0} | all-to-all | bytes 229376 | tf_op jit(solution)/shard_map/all_to_all | solution.py:208
  118.4 1.4 %unpack.1 = (bf16[448,128]{1,0:T(8,128)(2,1)}, bf16[128,512]{1,0:T(8,128)(2,1)}, bf16[128,512]{1,0:T(8,128)(2,1)}) custom-call(bf16[32,2,896]{2,1,0:T(2,128)(2,1)S(1)} %all_to_all.23.in_ref, bf16[128,512]{1,0:T(8,128)(2,1)S(1)} %get-tuple-element.16.att_ref, bf16[128,512]{1,0:T(8,128)(2,1)S(1)} %get-tuple-element.17.dq_ref), custom_call_target="tpu_custom_call" | custom-call | tf_op jit(solution)/shard_map/unpack/pallas_call | solution.py:260
  (3 shorter events, 0.0 us)
Async XLA Ops:
  0.6 0.9 copy-start.4
  61.5 5.0 %copy-start = (bf16[448,512]{1,0:T(8,128)(2,1)S(1)}, bf16[448,512]{1,0:T(8,128)(2,1)}, u32[]{:S(2)}) copy-start(bf16[448,512]{1,0:T(8,128)(2,1)} %wk_ref.1) | copy-start | bytes 1376260
  61.5 5.0 %copy-start.1 = (bf16[448,512]{1,0:T(8,128)(2,1)S(1)}, bf16[448,512]{1,0:T(8,128)(2,1)}, u32[]{:S(2)}) copy-start(bf16[448,512]{1,0:T(8,128)(2,1)} %wv_ref.1) | copy-start | bytes 1376260
  61.5 5.0 %copy-start.2 = (bf16[128,512]{1,0:T(8,128)(2,1)S(1)}, bf16[128,512]{1,0:T(8,128)(2,1)}, u32[]{:S(2)}) copy-start(bf16[128,512]{1,0:T(8,128)(2,1)} %q_ref.1) | copy-start | bytes 393220
  61.6 4.9 %copy-start.3 = (bf16[128,512]{1,0:T(8,128)(2,1)S(1)}, bf16[128,512]{1,0:T(8,128)(2,1)}, u32[]{:S(2)}) copy-start(bf16[128,512]{1,0:T(8,128)(2,1)} %g_ref.1) | copy-start | bytes 393220
  66.5 0.7 copy-start.5
  66.5 0.7 copy-start.6

commit v6 on v5

--- a/solution.py
+++ b/solution.py
@@ -14,7 +14,7 @@
 X_CHIPS = 4
 CORES = 2
 FIRST_IN = 20
-FIRST_OUT = 16
+FIRST_OUT = 18
 FIRST_X = 2
 FIRST_Y = 2
 BF = jnp.bfloat16

time: 121 us -> 120 us (level)
  no operation moved by 1% of the time
where the time goes in v6:
time: 120 us
  blocking collectives  109 us (91%)
  Pallas kernels  7.84 us (7%)
  local copies, waits for them, and re-layouts  1.56 us (1%)
    all_to_all x2, blocking collectives, exchange(): lax.all_to_all(messages, 'z', split_axis=0, concat_axis=0, axis_index_gro...  77.4 us
    all_to_all x2, blocking collectives, exchange_xy(): lax.all_to_all(messages, ('x', 'y'), split_axis=0, concat_axis=0, axis_in...  24.6 us
    pallas_call x1, Pallas kernels, per_device(): call(attend_kernel, (shape(*queries.shape), shape(*queries.shape), half,...  5.09 us
    all_gather x1, blocking collectives, per_device(): lax.all_gather(out, 'core', axis=0)  4.91 us
    all_gather x1, blocking collectives, per_device(): both = lax.all_gather(send.reshape(n_y, flat, NB_LEN), 'core', axis=0)  2.46 us

profile of v6, /device:TPU:1, one launch (start us, length us, event | category | flops | bytes accessed | tf_op | source)
XLA Modules:
  0.0 119.5 jit_solution(6859368973323152023)
XLA Ops:
  0.6 0.0 copy-start.4
  0.6 0.9 copy-done.4
  1.5 0.3 pack.1
  1.8 46.3 %all_to_all.20.in_ref = bf16[32,2,896]{2,1,0:T(2,128)(2,1)S(1)} all-to-all(bf16[32,2,896]{2,1,0:T(2,128)(2,1)S(1)} %pack.1), channel_id=1, replica_groups={{640,672,704,736,512,544,576,608,896,928,960,992,768,800,832,864,128,16..., dimensions={0} | all-to-all | bytes 229376 | tf_op jit(solution)/shard_map/all_to_all | solution.py:208
  48.1 0.2 spread.1
  48.4 12.7 %all_to_all.21 = bf16[16,16,896]{2,1,0:T(8,128)(2,1)S(1)} all-to-all(bf16[16,16,896]{2,1,0:T(8,128)(2,1)S(1)} %bitcast.16), channel_id=1, replica_groups={{20,22,16,18,28,30,24,26,4,6,0,2,12,14,8,10},{21,23,17,19,29,31,25,27,5..., dimensions={0} | all-to-all | bytes 917504 | tf_op jit(solution)/shard_map/all_to_all | solution.py:216
  61.1 0.4 turn.1
  61.5 0.0 copy-start
  61.5 0.0 copy-start.1
  61.5 0.0 copy-start.2
  61.6 0.0 copy-start.3
  61.6 4.9 %all-gather = bf16[8,448,128]{2,1,0:T(8,128)(2,1)S(1)} all-gather(bf16[4,448,128]{2,1,0:T(8,128)(2,1)S(1)} %turn.1), channel_id=2, replica_groups=mesh['z'=32,'x'=4,'y'=4,'core'=2] {'core'}, dimensions={0}, use_global_device_ids=true | all-gather | bytes 1376256 | tf_op jit(solution)/shard_map/all_gather | solution.py:240
  66.5 0.0 copy-done
  66.5 0.0 copy-done.1
  66.5 0.0 copy-done.2
  66.5 0.6 copy-done.5
  67.1 0.0 copy-done.6
  67.1 5.1 %attend.1 = (bf16[128,512]{1,0:T(8,128)(2,1)S(1)}, bf16[128,512]{1,0:T(8,128)(2,1)S(1)}, bf16[4,8,56,128]{3,2,1,0:T(8,128)(2,1)S(1)}, bf16[4,8,56,128]{3,2,1,0:T(8,128)(2,1)S(1)}) custom-call(s32[2]{0:T(128)S(1)} %copy-done.5, s32[1,8]{1,0:T(1,128)S(1)} %copy-done.6, s32[1]{0:T(128)} %bitcast.core_ref, bf16[2,4,8,56,128]{4,3,2,1,0:T(8,128)(2,1)S(1)} %bitcast.14, ...), custom_call_target="tpu_custom_call" | custom-call | tf_op jit(solution)/shard_map/attend/pallas_call | solution.py:242
  72.2 2.5 %all_gather.11.both_ref = bf16[2,4,448,128]{3,2,1,0:T(8,128)(2,1)S(1)} all-gather(bf16[1,4,448,128]{3,2,1,0:T(8,128)(2,1)S(1)} %bitcast.20), channel_id=1, replica_groups=mesh['z'=32,'x'=4,'y'=4,'core'=2] {'core'}, dimensions={0}, use_global_device_ids=true | all-gather | bytes 1376256 | tf_op jit(solution)/shard_map/all_gather | solution.py:255
  74.7 0.3 join.1
  75.0 11.9 %all_to_all.22 = bf16[16,16,896]{2,1,0:T(8,128)(2,1)S(1)} all-to-all(bf16[16,16,896]{2,1,0:T(8,128)(2,1)S(1)} %bitcast.18), channel_id=1, replica_groups={{20,22,16,18,28,30,24,26,4,6,0,2,12,14,8,10},{21,23,17,19,29,31,25,27,5..., dimensions={0} | all-to-all | bytes 917504 | tf_op jit(solution)/shard_map/all_to_all | solution.py:216
  86.9 0.2 sum.1
  87.1 31.1 %all_to_all.23.in_ref = bf16[32,2,896]{2,1,0:T(2,128)(2,1)S(1)} all-to-all(bf16[32,2,896]{2,1,0:T(2,128)(2,1)S(1)} %sum.1), channel_id=1, replica_groups={{576,608,512,544,704,736,640,672,832,864,768,800,960,992,896,928,64,96,..., dimensions={0} | all-to-all | bytes 229376 | tf_op jit(solution)/shard_map/all_to_all | solution.py:208
  118.1 1.4 %unpack.1 = (bf16[448,128]{1,0:T(8,128)(2,1)}, bf16[128,512]{1,0:T(8,128)(2,1)}, bf16[128,512]{1,0:T(8,128)(2,1)}) custom-call(bf16[32,2,896]{2,1,0:T(2,128)(2,1)S(1)} %all_to_all.23.in_ref, bf16[128,512]{1,0:T(8,128)(2,1)S(1)} %get-tuple-element.16.att_ref, bf16[128,512]{1,0:T(8,128)(2,1)S(1)} %get-tuple-element.17.dq_ref), custom_call_target="tpu_custom_call" | custom-call | tf_op jit(solution)/shard_map/unpack/pallas_call | solution.py:260
  (3 shorter events, 0.0 us)
Async XLA Ops:
  0.6 0.9 copy-start.4
  61.5 5.0 %copy-start = (bf16[448,512]{1,0:T(8,128)(2,1)S(1)}, bf16[448,512]{1,0:T(8,128)(2,1)}, u32[]{:S(2)}) copy-start(bf16[448,512]{1,0:T(8,128)(2,1)} %wk_ref.1) | copy-start | bytes 1376260
  61.5 5.0 %copy-start.1 = (bf16[448,512]{1,0:T(8,128)(2,1)S(1)}, bf16[448,512]{1,0:T(8,128)(2,1)}, u32[]{:S(2)}) copy-start(bf16[448,512]{1,0:T(8,128)(2,1)} %wv_ref.1) | copy-start | bytes 1376260
  61.5 5.0 %copy-start.2 = (bf16[128,512]{1,0:T(8,128)(2,1)S(1)}, bf16[128,512]{1,0:T(8,128)(2,1)}, u32[]{:S(2)}) copy-start(bf16[128,512]{1,0:T(8,128)(2,1)} %q_ref.1) | copy-start | bytes 393220
  61.6 4.9 %copy-start.3 = (bf16[128,512]{1,0:T(8,128)(2,1)S(1)}, bf16[128,512]{1,0:T(8,128)(2,1)}, u32[]{:S(2)}) copy-start(bf16[128,512]{1,0:T(8,128)(2,1)} %g_ref.1) | copy-start | bytes 393220
  66.5 0.7 copy-start.5
  66.5 0.7 copy-start.6
